TPU v7x, 512 devices: a whole 4x4x16 slice. The times are simulated.
512 devices in a mesh: grp: 16 (over y, x), ch: 32 (over z, core).
Axes of the slice: x: 4, y: 4, z: 16, core: 2. Of those that a mesh axis runs over, the one named last changes fastest.
Arguments:
- x_in: bfloat16 [65536, 8192], P(('grp', 'ch')), may hold values from -6 to 6
- bc_in: bfloat16 [65536, 256], P(('grp', 'ch')), may hold values from -6 to 6
- dt_in: bfloat16 [65536, 128], P(('grp', 'ch')), may hold values from -2 to 14
- dt_bias: float32 [128], replicated, may hold values from -3 to -1
- a_log: float32 [128], P('ch'), may hold values from -7.5 to 0
- skip_d: float32 [128], P('ch'), may hold values from 0.5 to 1.5
- conv_x: float32 [4, 8192], P(None, 'ch'), may hold values from -3 to 3
- conv_x_bias: float32 [8192], P('ch'), may hold values from -3 to 3
- conv_bc: float32 [4, 256], replicated, may hold values from -3 to 3
- conv_bc_bias: float32 [256], replicated, may hold values from -3 to 3
- norm_gain: float32 [8192], replicated, may hold values from 0.5 to 1.5
- lengths: int32 [256], replicated, may hold values from 64 to 256, as said below
- dest_group: int32 [256], replicated, may hold values from -1 to 15, as said below
- dest_slot: int32 [256], replicated, may hold values from -1 to 15, as said below
Outputs:
- mixer_out: bfloat16 [65536, 8192], P(('grp', 'ch'))
Inputs may be any that keep to these rules, and one draw needn't show every extreme that they name: `dest_group`: -1 marks a dropped pair. From one group at most 2 surviving pairs go to any one group, and every group sends exactly 2 to some group; one group's pairs go to at most 8 groups. `dest_slot`: -1 exactly where dest_group is -1; no two surviving pairs share a destination group and slot. `lengths`: every group holds at least one pair of length 256.
All inputs are finite; a program needn't handle non-finite values.
Results may differ from a plain program's by a relative error of at most 0.0053.
Values may be sent and summed in bfloat16 or wider, within the bound.
No kernel may reach another device: no remote copies, remote signals or barrier semaphores. Data moves between devices by JAX's collectives and lax.ppermute only.
A program may use at most 64 MiB of HBM per device.

v0:
```python
import functools

import jax
import jax.numpy as jnp
from jax import lax
from jax.experimental import pallas as pl
from jax.experimental.pallas import tpu as pltpu
from jax.sharding import PartitionSpec as P

LEVELS = (96, 128, 144, 152, 160, 168, 176, 184, 192, 200, 208, 224)
LOG2E = 1.4426950408889634
F32 = jnp.float32
BF16 = jnp.bfloat16


def conv_silu(values, taps, bias, rows):
    count = 4
    total = jnp.broadcast_to(bias, values.shape)
    for k in range(count):
        back = count - 1 - k
        moved = values
        if back:
            moved = jnp.where(rows >= back, pltpu.roll(values, back, 0), 0.0)
        total = total + taps[k : k + 1] * moved
    low = 0.5 * total
    return low + low * jnp.tanh(low)


def mix_kernel(
    heads, spread, sc, x_own, x_oth, bc_own, bc_oth, w, wbc, step, neg, out,
    scores, decay, pick, joint, joint_bc,
):
    core, used = sc[0], sc[1]
    j = pl.program_id(0)
    half, width = x_own.shape
    length = 2 * half

    def joined(own, oth, buffer):
        buffer[core] = own[...]
        buffer[1 - core] = oth[...]
        both = buffer[...].reshape(length, own.shape[1]).astype(F32)
        rows = lax.broadcasted_iota(jnp.int32, both.shape, 0)
        return jnp.where(rows < used, both, 0.0), rows

    @pl.when(j == 0)
    def _():
        bc, rows = joined(bc_own, bc_oth, joint_bc)
        act = conv_silu(bc, wbc[0:4], wbc[4:5], rows)
        state = act.shape[1] // 2
        later = lax.broadcasted_iota(jnp.int32, (length, length), 0)
        earlier = lax.broadcasted_iota(jnp.int32, (length, length), 1)
        raw = lax.dot_general(
            act[:, state:],
            act[:, :state],
            (((1,), (1,)), ((), ())),
            precision=lax.Precision.HIGHEST,
            preferred_element_type=F32,
        )
        scores[...] = jnp.where(later >= earlier, raw, 0.0)
        upper = jnp.where(later <= earlier, 1.0, 0.0).astype(F32)
        decay[...] = LOG2E * jnp.dot(
            neg[...], upper, precision=lax.Precision.HIGHEST, preferred_element_type=F32
        )
        keep = length // spread
        place = (later % keep) * spread + later // keep
        pick[...] = jnp.where(earlier == place, 1.0, 0.0).astype(BF16)

    x, rows = joined(x_own, x_oth, joint)
    x_act = conv_silu(x, w[0, 0:4], w[0, 4:5], rows)
    at = pl.ds(pl.multiple_of(8 * j, 8), 8)
    decay_rows = decay[at]
    decay_cols = jnp.transpose(decay_rows)
    step_cols = jnp.transpose(step[at])
    dim = width // heads
    pair = 2 * dim
    first = lax.broadcasted_iota(jnp.int32, (length, pair), 1) < dim
    mixed = []
    for p in range(heads // 2):
        steps = jnp.where(
            first, step_cols[:, 2 * p : 2 * p + 1], step_cols[:, 2 * p + 1 : 2 * p + 2]
        )
        fed = x_act[:, p * pair : (p + 1) * pair] * steps
        fed_hi = fed.astype(BF16)
        fed_lo = (fed - fed_hi.astype(F32)).astype(BF16)
        fed_both = jnp.concatenate([fed_hi, fed_lo], axis=1)
        sums = []
        for h in (2 * p, 2 * p + 1):
            parts = []
            for lo, hi in ((0, half), (half, length)):
                gap = decay_cols[lo:hi, h : h + 1] - decay_rows[h : h + 1, :hi]
                weight = scores[lo:hi, :hi] * jnp.exp2(jnp.minimum(gap, 0.0))
                both = jnp.dot(weight.astype(BF16), fed_both[:hi], preferred_element_type=F32)
                parts.append(both[:, :pair] + both[:, pair:])
            sums.append(jnp.concatenate(parts, axis=0))
        mixed.append(jnp.where(first, sums[0], sums[1]))
    result = jnp.concatenate(mixed, axis=1) + w[0, 5:6] * x_act
    out[0] = jnp.dot(pick[...], result.astype(BF16), preferred_element_type=F32).astype(BF16)


def one_hot(size, place):
    at = lax.broadcasted_iota(jnp.int32, (size, place.shape[1]), 0)
    return jnp.where(at == place, 1.0, 0.0).astype(BF16)


def one_hot_back(size, place):
    count = place.shape[1]
    column = jnp.transpose(jnp.broadcast_to(place.astype(F32), (8, count)))[:, :1]
    at = lax.broadcasted_iota(jnp.int32, (count, size), 1).astype(F32)
    return jnp.where(at == column, 1.0, 0.0).astype(BF16)


def chosen(pick, rows):
    return jnp.dot(pick, rows, preferred_element_type=F32).astype(BF16)


def pack_kernel(sc, rows, place, out, pick):
    @pl.when(pl.program_id(0) == 0)
    def _():
        pick[...] = one_hot(out.shape[1], place[0])

    out[0] = chosen(pick[...], rows[...].reshape(place.shape[2], rows.shape[2]))


def widen_kernel(rows, place, out):
    one = chosen(one_hot_back(rows.shape[1], place[0]), rows[0])
    out[0] = one.reshape(out.shape[1:])


def order_kernel(count, source, rows, place, out):
    z = pl.program_id(0)
    blocks = []
    for g in range(count):
        i = source[z * count + g]
        blocks.append(rows[i // count, i % count])
    out[0] = chosen(one_hot(out.shape[1], place[0]), jnp.concatenate(blocks, axis=0))


def unpack_kernel(sc, rows, place, out, pick):
    @pl.when(pl.program_id(0) == 0)
    def _():
        pick[...] = one_hot_back(rows.shape[1], place[0])

    out[...] = chosen(pick[...], rows[0]).reshape(out.shape)


def finish_kernel(spread, sc, rows, own, oth, pick):
    core, last, filled = sc[0], sc[1], sc[2]
    length = rows.shape[1]
    half = length // 2
    keep = length // spread

    @pl.when(pl.program_id(0) == 0)
    def _():
        source = lax.broadcasted_iota(jnp.int32, (length, length), 1)
        index = lax.broadcasted_iota(jnp.int32, (length, length), 0)
        swapped = jnp.where(index < half, index + half, index - half)
        t = jnp.minimum(jnp.where(core == 0, index, swapped), last)
        place = (t % spread) * keep + t // spread
        pick[...] = jnp.where((source == place) & (filled > 0), 1.0, 0.0).astype(BF16)

    picked = chosen(pick[...], rows[0])
    own[...] = picked[:half]
    oth[...] = picked[half:]


def norm_kernel(sc, own, oth, gain, out):
    core = sc[0]
    width = own.shape[1]
    mine, other = own[...].astype(F32), oth[...].astype(F32)
    total = jnp.sum(mine * mine, axis=1, keepdims=True) + jnp.sum(
        other * other, axis=1, keepdims=True
    )
    scale = lax.rsqrt(total / (2 * width) + 1e-05)
    for values, side in ((mine, core), (other, 1 - core)):
        at = pl.ds(pl.multiple_of(side * width, width), width)
        out[:, at] = (values * scale * gain[:, at]).astype(BF16)


def grid_spec(scalars, grid, ins, outs, scratch=()):
    return pltpu.PrefetchScalarGridSpec(
        num_scalar_prefetch=scalars,
        grid=grid,
        in_specs=ins,
        out_specs=outs,
        scratch_shapes=list(scratch),
    )


def whole(shape):
    return pl.BlockSpec(shape, lambda *_: (0,) * len(shape))


def per_device(
    x_in,
    bc_in,
    dt_in,
    dt_bias,
    a_log,
    skip_d,
    conv_x,
    conv_x_bias,
    conv_bc,
    conv_bc_bias,
    norm_gain,
    lengths,
    dest_group,
    dest_slot,
):
    n_ch = lax.axis_size("ch")
    n_grp = lax.axis_size("grp")
    n_z = n_ch // 2
    me = lax.axis_index("ch")
    my_group = lax.axis_index("grp")
    my_z, core = me // 2, me % 2
    half, channels = x_in.shape
    length = 2 * half
    mine = channels // 2
    width = channels // n_ch
    heads = a_log.shape[0]
    head_dim = width // heads
    head_half = dt_in.shape[1] // 2
    chunks = mine // width
    keep = length // n_z
    swap = [(i, i ^ 1) for i in range(n_ch)]
    rings = [[2 * z + c for z in range(n_z)] for c in range(2)]

    other_half = 1 - core
    x_oth = lax.ppermute(
        lax.dynamic_slice_in_dim(x_in, other_half * mine, mine, 1), "ch", swap
    )
    bc_oth = lax.ppermute(bc_in, "ch", swap)
    dt_oth = lax.ppermute(
        lax.dynamic_slice_in_dim(dt_in, other_half * head_half, head_half, 1), "ch", swap
    )
    small = jnp.concatenate(
        [
            conv_x,
            conv_x_bias[None],
            jnp.repeat(skip_d, head_dim)[None],
            jnp.repeat(a_log, head_dim)[None],
            jnp.zeros((1, width), F32),
        ],
        axis=0,
    )
    small_oth = lax.ppermute(small, "ch", swap)
    shares = jnp.stack(
        [jnp.where(core == 0, small, small_oth), jnp.where(core == 0, small_oth, small)]
    )

    def exchange(a):
        return lax.all_to_all(
            a, "ch", split_axis=0, concat_axis=0, axis_index_groups=rings, tiled=True
        )

    w_all = exchange(jnp.broadcast_to(shares[None], (n_z, 2, 8, width))).reshape(n_ch, 8, width)

    pairs = n_grp * n_z
    ids = jnp.arange(pairs, dtype=jnp.int32)
    alive = dest_group >= 0
    units = jnp.where(alive, (jnp.minimum(lengths + 4, length) + n_z - 1) // n_z, 0)
    by_group = units.reshape(n_grp, n_z)
    ends = jnp.cumsum(by_group, axis=0)
    starts = ends - by_group
    target = jnp.where(alive, dest_group * n_z + dest_slot, pairs)
    match = target[None, :] == ids[:, None]

    def looked_up(values):
        return jnp.sum(jnp.where(match, values[None, :], 0), axis=1)

    to_units = looked_up(units).reshape(n_grp, n_z)
    slot_len = looked_up(lengths)
    source = looked_up((ids % n_z) * n_grp + ids // n_z)
    to_ends = jnp.cumsum(to_units, axis=0)
    to_starts = to_ends - to_units

    def places(count, start):
        k = jnp.arange(keep, dtype=jnp.int32)
        at = jnp.where(k < count.T[:, :, None], start.T[:, :, None] + k, -1)
        return at.reshape(n_z, 1, n_grp * keep)

    place_from = places(by_group, starts)
    place_to = places(to_units, to_starts)
    source = source.reshape(n_grp, n_z).T.reshape(-1)
    z_only = my_z[None].astype(jnp.int32)

    my_dt = lax.dynamic_slice_in_dim(dt_in, core * head_half, head_half, 1)
    dt_both = jnp.concatenate(
        [jnp.where(core == 0, my_dt, dt_oth), jnp.where(core == 0, dt_oth, my_dt)], axis=0
    )
    used = lengths[my_group * n_z + my_z]
    valid = jnp.arange(length, dtype=jnp.int32) < used
    bias = lax.dynamic_slice_in_dim(dt_bias, core * head_half, head_half, 0)
    step = (
        jax.nn.softplus(dt_both.astype(F32) + bias[None, :]) * valid[:, None].astype(F32)
    ).astype(BF16).astype(F32)
    rate_all = jnp.exp(w_all[:, 6, ::head_dim])
    rate = lax.dynamic_slice_in_dim(rate_all, core * chunks, chunks, 0)

    def by_chunk(a):
        a = a.reshape(chunks, heads, length)
        return jnp.pad(a, ((0, 0), (0, 8 - heads), (0, 0))).reshape(chunks * 8, length)

    step_t = by_chunk(step.T)
    neg_t = by_chunk(-step.T * rate.reshape(-1)[:, None])
    wbc = jnp.concatenate([conv_bc, conv_bc_bias[None], jnp.zeros((3, conv_bc.shape[1]), F32)], axis=0)

    mixed = pl.pallas_call(
        functools.partial(mix_kernel, heads, n_z),
        out_shape=jax.ShapeDtypeStruct((chunks, length, width), BF16),
        grid_spec=grid_spec(
            1,
            (chunks,),
            [
                pl.BlockSpec((half, width), lambda j, sc: (0, sc[0] * chunks + j)),
                pl.BlockSpec((half, width), lambda j, sc: (0, j)),
                whole(bc_in.shape),
                whole(bc_in.shape),
                pl.BlockSpec((1, 8, width), lambda j, sc: (sc[0] * chunks + j, 0, 0)),
                whole(wbc.shape),
                whole(step_t.shape),
                whole(neg_t.shape),
            ],
            pl.BlockSpec((1, length, width), lambda j, sc: (j, 0, 0)),
            [
                pltpu.VMEM((length, length), F32),
                pltpu.VMEM((chunks * 8, length), F32),
                pltpu.VMEM((length, length), BF16),
                pltpu.VMEM((2, half, width), BF16),
                pltpu.VMEM((2,) + bc_in.shape, BF16),
            ],
        ),
        name="mix",
    )(jnp.stack([core, used]).astype(jnp.int32), x_in, x_oth, bc_in, bc_oth, w_all, wbc, step_t, neg_t)

    spread = lax.all_to_all(mixed, "grp", split_axis=0, concat_axis=0, tiled=True)

    full = n_grp * keep
    my_place = pl.BlockSpec((1, 1, full), lambda i, sc: (sc[0], 0, 0))
    each_place = pl.BlockSpec((1, 1, full), lambda i, *_: (i, 0, 0))
    strided = pl.BlockSpec((n_grp, keep, width), lambda i, *_: (0, i, 0))
    wide_shape = (n_z, n_grp, keep, width)

    def by_z(size):
        return pl.BlockSpec((1, size, width), lambda i, *_: (i, 0, 0))

    def short(size):
        return jax.ShapeDtypeStruct((n_z, size, width), BF16)

    def outward(size, spread):
        outgoing = pl.pallas_call(
            pack_kernel,
            out_shape=short(size),
            grid_spec=grid_spec(
                1, (n_z,), [strided, my_place], by_z(size), [pltpu.VMEM((size, full), BF16)]
            ),
            name="pack",
        )(z_only, spread, place_from)
        return pl.pallas_call(
            widen_kernel,
            out_shape=jax.ShapeDtypeStruct(wide_shape, BF16),
            grid_spec=grid_spec(
                0,
                (n_z,),
                [by_z(size), each_place],
                pl.BlockSpec((1,) + wide_shape[1:], lambda i: (i, 0, 0, 0)),
            ),
            name="widen",
        )(exchange(outgoing), place_from)

    def homeward(size, wide):
        ordered = pl.pallas_call(
            functools.partial(order_kernel, n_grp),
            out_shape=short(size),
            grid_spec=grid_spec(1, (n_z,), [whole(wide_shape), each_place], by_z(size)),
            name="order",
        )(source, wide, place_to)
        return pl.pallas_call(
            unpack_kernel,
            out_shape=jax.ShapeDtypeStruct((n_grp, length, width), BF16),
            grid_spec=grid_spec(
                1, (n_z,), [by_z(size), my_place], strided, [pltpu.VMEM((full, size), BF16)]
            ),
            name="unpack",
        )(z_only, exchange(ordered), place_to)

    sizes = [s for s in LEVELS if s < full] + [full]

    def sized(step, needed, rows):
        level = jnp.sum((jnp.max(needed) > jnp.array(sizes[:-1], jnp.int32)).astype(jnp.int32))
        return lax.switch(level, [functools.partial(step, s) for s in sizes], rows)

    wide = sized(outward, ends[-1], spread)
    landed = sized(homeward, to_ends[-1], wide)
    rows = lax.all_to_all(landed, "grp", split_axis=0, concat_axis=0, tiled=True)

    slot = my_group * n_z + my_z
    last = jnp.minimum(slot_len[slot] + 3, length - 1)
    filled = jnp.any(target == slot)
    ends_at = jnp.stack([core, last, filled.astype(jnp.int32)]).astype(jnp.int32)
    own, oth = pl.pallas_call(
        functools.partial(finish_kernel, n_z),
        out_shape=[jax.ShapeDtypeStruct((half, mine), BF16)] * 2,
        grid_spec=grid_spec(
            1,
            (chunks,),
            [pl.BlockSpec((1, length, width), lambda j, sc: (j, 0, 0))],
            [pl.BlockSpec((half, width), lambda j, sc: (0, j))] * 2,
            [pltpu.VMEM((length, length), BF16)],
        ),
        name="finish",
    )(ends_at, rows)
    got = lax.ppermute(oth, "ch", swap)
    step_rows = 32
    return pl.pallas_call(
        norm_kernel,
        out_shape=jax.ShapeDtypeStruct((half, channels), BF16),
        grid_spec=grid_spec(
            1,
            (half // step_rows,),
            [pl.BlockSpec((step_rows, mine), lambda i, sc: (i, 0))] * 2 + [whole((1, channels))],
            pl.BlockSpec((step_rows, channels), lambda i, sc: (i, 0)),
        ),
        name="norm",
    )(ends_at, own, got, norm_gain[None])


def solution(mesh):
    placed = (
        P(("grp", "ch"), None),
        P(("grp", "ch"), None),
        P(("grp", "ch"), None),
        P(),
        P("ch"),
        P("ch"),
        P(None, "ch"),
        P("ch"),
        P(),
        P(),
        P(),
        P(),
        P(),
        P(),
    )
    return jax.shard_map(
        per_device, mesh=mesh, in_specs=placed, out_specs=P(("grp", "ch"), None), check_vma=False
    )
```

profile of v0, /device:TPU:1, one launch (start us, length us, event | category | flops | bytes accessed | tf_op | source)
XLA Modules:
  0.0 359.9 jit_solution(6695083952253836145)
XLA Ops:
  0.0 0.8 broadcast_in_dim.88
  0.8 0.1 broadcast_in_dim_reshape.8
  0.9 0.7 broadcast_in_dim.87
  1.6 0.1 broadcast_in_dim_reshape.7
  1.7 0.7 concatenate.9
  2.4 8.7 %collective-permute-start.2 = (f32[8,256]{1,0:T(8,128)S(1)}, f32[8,256]{1,0:T(8,128)S(1)}, u32[]{:S(2)}, u32[]{:S(2)}) collective-permute-start(f32[8,256]{1,0:T(8,128)S(1)} %concatenate.9), channel_id=1, source_target_pairs={{0,1},{1,0},{2,3},{3,2},{4,5},{5,4},{6,7},{7,6},{8,9},{9,8},{10,11... | collective-permute-start | bytes 24584 | tf_op jit(solution)/shard_map/ppermute | solution.py:245
  11.2 0.9 constant_dynamic-slice_fusion.1
  12.1 0.1 copy.177
  12.2 1.9 collective-permute-start.3
  14.1 2.4 collective-permute-start.1
  16.5 1.3 constant_dynamic-slice_fusion.2
  17.9 1.9 collective-permute-start
  19.8 0.6 dynamic_slice.22
  20.5 0.7 broadcast_in_dim.90
  21.3 9.6 %all-to-all-start.26 = ((f32[16,2,8,256]{3,2,1,0:T(8,128)}), f32[16,2,8,256]{3,2,1,0:T(8,128)S(1)}, u32[]{:S(2)}, u32[]{:S(2)}) async-start(f32[16,2,8,256]{3,2,1,0:T(8,128)} %broadcast_in_dim.90), calls=%async_computation.26 | async-start | bytes 524288 | tf_op jit(solution)/shard_map/all_to_all | solution.py:251
  30.9 0.7 maximum_maximum_fusion.wbc
  31.5 0.6 compare_convert_fusion
  32.1 1.2 pad_add_fusion.1.sc
  33.4 0.1 copy.176
  33.5 0.1 convert_bitcast_fusion
  33.7 0.7 pad_bitcast_fusion.1.step
  34.3 10.3 %all-to-all-done.26 = f32[16,2,8,256]{3,2,1,0:T(8,128)S(1)} async-done(((f32[16,2,8,256]{3,2,1,0:T(8,128)}), f32[16,2,8,256]{3,2,1,0:T(8,128)S(1)}, u32[]{:S(2)}, u32[]{:S(2)}) %all-to-all-start.26) | async-done | bytes 262176 | tf_op jit(solution)/shard_map/all_to_all | solution.py:251
  44.7 0.2 slice.11
  44.9 0.1 mul.54
  45.0 0.1 negate_multiply_fusion
  45.2 0.7 pad_bitcast_fusion.neg
  45.9 0.6 copy-done.5
  46.5 1.0 copy-done.4
  47.5 18.6 %mix.1 = bf16[16,256,256]{2,1,0:T(8,128)(2,1)} custom-call(s32[2]{0:T(128)} %pad_add_fusion.1.sc, bf16[128,8192]{1,0:T(8,128)(2,1)} %x_own.1, bf16[128,4096]{1,0:T(8,128)(2,1)} %copy-done.4, bf16[128,256]{1,0:T(8,128)(2,1)} %bc_own.1, bf16[128,256]{1,0:T(8,128)(2,1)} %copy-done.5, f32[32,8,256]{2,1,0:T(8,128)} %bitcast.54, ...), custom_call_target="tpu_custom_call" | custom-call | tf_op jit(solution)/shard_map/mix/pallas_call | solution.py:307
  66.0 6.9 %all-to-all-start.27 = ((bf16[16,256,256]{2,1,0:T(8,128)(2,1)}), bf16[16,256,256]{2,1,0:T(8,128)(2,1)S(1)}, u32[]{:S(2)}, u32[]{:S(2)}) async-start(bf16[16,256,256]{2,1,0:T(8,128)(2,1)} %mix.1), calls=%async_computation.27 | async-start | bytes 4194304 | tf_op jit(solution)/shard_map/all_to_all | solution.py:335
  73.1 0.6 compare_reduce_fusion
  73.7 0.2 select_reduce_fusion
  74.2 0.7 slice_reduce_fusion
  75.0 1.9 fusion.9
  78.3 0.1 lt.416
  78.4 0.1 lt.417
  78.5 0.1 add.295
  78.6 0.1 add.296
  78.8 18.3 %all-to-all-done.27 = bf16[16,256,256]{2,1,0:T(8,128)(2,1)S(1)} async-done(((bf16[16,256,256]{2,1,0:T(8,128)(2,1)}), bf16[16,256,256]{2,1,0:T(8,128)(2,1)S(1)}, u32[]{:S(2)}, u32[]{:S(2)}) %all-to-all-start.27) | async-done | bytes 2097184 | tf_op jit(solution)/shard_map/all_to_all | solution.py:335
  97.1 101.2 %conditional.2 = (bf16[16,16,16,256]{3,2,1,0:T(8,128)(2,1)S(1)}) conditional(s32[]{:T(128)} %clamp.7, (s32[1]{0:T(128)}, bf16[16,256,256]{2,1,0:T(8,128)(2,1)S(1)}, s32[16,1,256]{2,1,0:T(1,128)S(1)}) %tuple.84, (s32[1]{0:T(128)}, bf16[16,256,256]{2,1,0:T(8,128)(2,1)S(1)}, s32[16,1,256]{2,1,0:T(1,128)S(1)}) %tuple.84, ...), branch_computations={%region_10.11_spmd, %region_11.12_spmd, %region_12.13_spmd, %regio... | conditional | bytes 4194312 | solution.py:390
  97.1 6.9 %pack.21 = bf16[16,192,256]{2,1,0:T(8,128)(2,1)} custom-call(s32[1]{0:T(128)} %get-tuple-element.460.sc, bf16[16,256,256]{2,1,0:T(8,128)(2,1)S(1)} %get-tuple-element.461.rows, s32[16,1,256]{2,1,0:T(1,128)S(1)} %get-tuple-element.462.place), custom_call_target="tpu_custom_call" | custom-call | tf_op jit(solution)/shard_map/cond/branch_8_fun/pack/pallas_call | solution.py:350
  104.0 83.6 %all_to_all.127.rows = bf16[16,192,256]{2,1,0:T(8,128)(2,1)} all-to-all(bf16[16,192,256]{2,1,0:T(8,128)(2,1)} %pack.21), channel_id=1, replica_groups={{0,2,4,6,8,10,12,14,16,18,20,22,24,26,28,30},{1,3,5,7,9,11,13,15,17,19,..., dimensions={0} | all-to-all | bytes 3145728 | tf_op jit(solution)/shard_map/cond/branch_8_fun/all_to_all | solution.py:251
  187.6 10.7 %widen.21 = bf16[16,16,16,256]{3,2,1,0:T(8,128)(2,1)S(1)} custom-call(bf16[16,192,256]{2,1,0:T(8,128)(2,1)} %all_to_all.127.rows, s32[16,1,256]{2,1,0:T(1,128)S(1)} %get-tuple-element.462.place), custom_call_target="tpu_custom_call" | custom-call | tf_op jit(solution)/shard_map/cond/branch_8_fun/widen/pallas_call | solution.py:358
  198.3 100.5 %conditional.3 = (bf16[16,256,256]{2,1,0:T(8,128)(2,1)S(1)}) conditional(s32[]{:T(128)} %clamp.6, (s32[16,16]{0,1:T(8,128)S(1)}, s32[256]{0:T(256)S(1)}, s32[256]{0:T(256)S(1)}, s32[16,16]{0,1:T(8,128)S(1)}, s32[16,16]{0,1:T(8,128)S(1)}, /*index=5*/s32[16,1,256]{2,1,0:T(1,128)S(1)}, ...), branch_computations={%region_23.24_spmd, %region_24.25_spmd, %region_25.26_spmd, %regio... | conditional | flops 12288 | bytes 4370440 | solution.py:390
  198.8 0.7 reshape.749.source
  199.5 0.1 lt.305
  199.6 0.1 lt.306
  199.7 0.1 add.238
  199.8 0.1 add.239
  199.9 0.6 compare_select_fusion.7.place
  200.5 10.0 %order.20 = bf16[16,184,256]{2,1,0:T(8,128)(2,1)} custom-call(s32[256]{0:T(256)} %reshape.749.source, bf16[16,16,16,256]{3,2,1,0:T(8,128)(2,1)S(1)} %get-tuple-element.533.rows, s32[16,1,256]{2,1,0:T(1,128)} %compare_select_fusion.7.place), custom_call_target="tpu_custom_call" | custom-call | tf_op jit(solution)/shard_map/cond/branch_7_fun/order/pallas_call | solution.py:371
  210.6 79.0 %all_to_all.139.rows = bf16[16,184,256]{2,1,0:T(8,128)(2,1)} all-to-all(bf16[16,184,256]{2,1,0:T(8,128)(2,1)} %order.20), channel_id=1, replica_groups={{0,2,4,6,8,10,12,14,16,18,20,22,24,26,28,30},{1,3,5,7,9,11,13,15,17,19,..., dimensions={0} | all-to-all | bytes 3014656 | tf_op jit(solution)/shard_map/cond/branch_7_fun/all_to_all | solution.py:251
  289.5 9.3 %unpack.20 = bf16[16,256,256]{2,1,0:T(8,128)(2,1)S(1)} custom-call(s32[1]{0:T(128)} %get-tuple-element.531.sc, bf16[16,184,256]{2,1,0:T(8,128)(2,1)} %all_to_all.139.rows, s32[16,1,256]{2,1,0:T(1,128)} %compare_select_fusion.7.place), custom_call_target="tpu_custom_call" | custom-call | tf_op jit(solution)/shard_map/cond/branch_7_fun/unpack/pallas_call | solution.py:377
  298.8 1.3 copy-done.1
  300.1 4.8 %all-to-all-start.28 = ((bf16[16,256,256]{2,1,0:T(8,128)(2,1)}), bf16[16,256,256]{2,1,0:T(8,128)(2,1)S(1)}, u32[]{:S(2)}, u32[]{:S(2)}) async-start(bf16[16,256,256]{2,1,0:T(8,128)(2,1)} %copy-done.1), calls=%async_computation.28 | async-start | bytes 4194304 | tf_op jit(solution)/shard_map/all_to_all | solution.py:394
  305.5 0.7 dynamic_slice.21
  306.8 0.6 pad_add_fusion.sc
  307.4 20.8 %all-to-all-done.28.rows = bf16[16,256,256]{2,1,0:T(8,128)(2,1)S(1)} async-done(((bf16[16,256,256]{2,1,0:T(8,128)(2,1)}), bf16[16,256,256]{2,1,0:T(8,128)(2,1)S(1)}, u32[]{:S(2)}, u32[]{:S(2)}) %all-to-all-start.28) | async-done | bytes 2097184 | tf_op jit(solution)/shard_map/all_to_all | solution.py:394
  328.2 1.3 copy-done
  329.5 11.5 %finish.1 = (bf16[128,4096]{1,0:T(8,128)(2,1)}, bf16[128,4096]{1,0:T(8,128)(2,1)}) custom-call(s32[3]{0:T(128)} %pad_add_fusion.sc, bf16[16,256,256]{2,1,0:T(8,128)(2,1)} %copy-done), custom_call_target="tpu_custom_call" | custom-call | tf_op jit(solution)/shard_map/finish/pallas_call | solution.py:400
  341.0 10.5 %collective-permute-start.4 = (bf16[128,4096]{1,0:T(8,128)(2,1)}, bf16[128,4096]{1,0:T(8,128)(2,1)S(1)}, u32[]{:S(2)}, u32[]{:S(2)}) collective-permute-start(bf16[128,4096]{1,0:T(8,128)(2,1)} %get-tuple-element.582), channel_id=1, source_target_pairs={{0,1},{1,0},{2,3},{3,2},{4,5},{5,4},{6,7},{7,6},{8,9},{9,8},{10,11... | collective-permute-start | bytes 3145736 | tf_op jit(solution)/shard_map/ppermute | solution.py:412
  351.5 2.5 collective-permute-done.4.oth
  354.0 1.0 copy-done.3
  354.9 5.0 %norm.1 = bf16[128,8192]{1,0:T(8,128)(2,1)} custom-call(s32[3]{0:T(128)} %pad_add_fusion.sc, bf16[128,4096]{1,0:T(8,128)(2,1)} %get-tuple-element.581.own, bf16[128,4096]{1,0:T(8,128)(2,1)} %copy-done.3, f32[1,8192]{1,0:T(1,128)} %bitcast.56), custom_call_target="tpu_custom_call" | custom-call | tf_op jit(solution)/shard_map/norm/pallas_call | solution.py:414
  (53 shorter events, 1.1 us)
Async XLA Ops:
  0.0 19.8 %copy-start.7 = (s32[256]{0:T(256)S(1)}, s32[256]{0:T(256)}, u32[]{:S(2)}) copy-start(s32[256]{0:T(256)} %param.53) | copy-start | bytes 3076
  0.0 30.8 %copy-start.9 = (f32[256]{0:T(256)S(1)}, f32[256]{0:T(256)}, u32[]{:S(2)}) copy-start(f32[256]{0:T(256)} %param.51) | copy-start | bytes 3076
  0.0 30.8 %copy-start.6 = (f32[4,256]{1,0:T(4,128)S(1)}, f32[4,256]{1,0:T(4,128)}, u32[]{:S(2)}) copy-start(f32[4,256]{1,0:T(4,128)} %param.50) | copy-start | bytes 12292
  0.0 33.3 %copy-start.12 = (f32[128]{0:T(128)S(1)}, f32[128]{0:T(128)}, u32[]{:S(2)}) copy-start(f32[128]{0:T(128)} %param.45) | copy-start | bytes 1540
  2.4 18.1 %collective-permute-start.2 = (f32[8,256]{1,0:T(8,128)S(1)}, f32[8,256]{1,0:T(8,128)S(1)}, u32[]{:S(2)}, u32[]{:S(2)}) collective-permute-start(f32[8,256]{1,0:T(8,128)S(1)} %concatenate.9), channel_id=1, source_target_pairs={{0,1},{1,0},{2,3},{3,2},{4,5},{5,4},{6,7},{7,6},{8,9},{9,8},{10,11... | collective-permute-start | bytes 24584 | tf_op jit(solution)/shard_map/ppermute | solution.py:245
  12.2 21.3 %collective-permute-start.3 = (bf16[128,64]{0,1:T(8,128)(2,1)S(1)}, bf16[128,64]{0,1:T(8,128)(2,1)S(1)}, u32[]{:S(2)}, u32[]{:S(2)}) collective-permute-start(bf16[128,64]{0,1:T(8,128)(2,1)S(1)} %copy.177), channel_id=1, source_target_pairs={{0,1},{1,0},{2,3},{3,2},{4,5},{5,4},{6,7},{7,6},{8,9},{9,8},{10,11... | collective-permute-start | bytes 49160 | tf_op jit(solution)/shard_map/ppermute | solution.py:232
  14.1 31.7 %collective-permute-start.1 = (bf16[128,256]{1,0:T(8,128)(2,1)}, bf16[128,256]{1,0:T(8,128)(2,1)S(1)}, u32[]{:S(2)}, u32[]{:S(2)}) collective-permute-start(bf16[128,256]{1,0:T(8,128)(2,1)} %bc_own.1), channel_id=1, source_target_pairs={{0,1},{1,0},{2,3},{3,2},{4,5},{5,4},{6,7},{7,6},{8,9},{9,8},{10,11... | collective-permute-start | bytes 196616 | tf_op jit(solution)/shard_map/ppermute | solution.py:231
  17.9 28.0 %collective-permute-start = (bf16[128,4096]{1,0:T(8,128)(2,1)S(1)}, bf16[128,4096]{1,0:T(8,128)(2,1)S(1)}, u32[]{:S(2)}, u32[]{:S(2)}) collective-permute-start(bf16[128,4096]{1,0:T(8,128)(2,1)S(1)} %constant_dynamic-slice_fusion.2), channel_id=1, source_target_pairs={{0,1},{1,0},{2,3},{3,2},{4,5},{5,4},{6,7},{7,6},{8,9},{9,8},{10,11... | collective-permute-start | bytes 3145736 | tf_op jit(solution)/shard_map/ppermute | solution.py:228
  21.3 23.4 %all-to-all-start.26 = ((f32[16,2,8,256]{3,2,1,0:T(8,128)}), f32[16,2,8,256]{3,2,1,0:T(8,128)S(1)}, u32[]{:S(2)}, u32[]{:S(2)}) async-start(f32[16,2,8,256]{3,2,1,0:T(8,128)} %broadcast_in_dim.90), calls=%async_computation.26 | async-start | bytes 524288 | tf_op jit(solution)/shard_map/all_to_all | solution.py:251
  44.7 1.2 copy-start.2
  45.9 0.6 copy-start.5
  46.5 1.0 copy-start.4
  66.0 6.9 %copy-start.8 = (s32[256]{0:T(256)S(1)}, s32[256]{0:T(256)}, u32[]{:S(2)}) copy-start(s32[256]{0:T(256)} %param.54) | copy-start | bytes 3076
  66.0 7.0 %copy-start.10 = (s32[256]{0:T(256)S(1)}, s32[256]{0:T(256)}, u32[]{:S(2)}) copy-start(s32[256]{0:T(256)} %param.55) | copy-start | bytes 3076
  66.0 8.9 %copy-start.11 = (s32[12]{0:T(128)S(1)}, s32[12]{0:T(128)}, u32[]{:S(2)}) copy-start(s32[12]{0:T(128)} %constant.115.clone) | copy-start | bytes 148
  66.0 31.1 %all-to-all-start.27 = ((bf16[16,256,256]{2,1,0:T(8,128)(2,1)}), bf16[16,256,256]{2,1,0:T(8,128)(2,1)S(1)}, u32[]{:S(2)}, u32[]{:S(2)}) async-start(bf16[16,256,256]{2,1,0:T(8,128)(2,1)} %mix.1), calls=%async_computation.27 | async-start | bytes 4194304 | tf_op jit(solution)/shard_map/all_to_all | solution.py:335
  298.8 1.3 copy-start.1
  300.1 28.0 %all-to-all-start.28 = ((bf16[16,256,256]{2,1,0:T(8,128)(2,1)}), bf16[16,256,256]{2,1,0:T(8,128)(2,1)S(1)}, u32[]{:S(2)}, u32[]{:S(2)}) async-start(bf16[16,256,256]{2,1,0:T(8,128)(2,1)} %copy-done.1), calls=%async_computation.28 | async-start | bytes 4194304 | tf_op jit(solution)/shard_map/all_to_all | solution.py:394
  328.2 1.3 copy-start
  341.0 13.0 %collective-permute-start.4 = (bf16[128,4096]{1,0:T(8,128)(2,1)}, bf16[128,4096]{1,0:T(8,128)(2,1)S(1)}, u32[]{:S(2)}, u32[]{:S(2)}) collective-permute-start(bf16[128,4096]{1,0:T(8,128)(2,1)} %get-tuple-element.582), channel_id=1, source_target_pairs={{0,1},{1,0},{2,3},{3,2},{4,5},{5,4},{6,7},{7,6},{8,9},{9,8},{10,11... | collective-permute-start | bytes 3145736 | tf_op jit(solution)/shard_map/ppermute | solution.py:412
  354.0 1.0 copy-start.3
where the time goes:
time: 361 us; the launch traced here: 360 us
  blocking collectives  163 us (45%)
  Pallas kernels  71.9 us (20%)
  waiting for transfers between devices  51.9 us (14%)
  starting transfers between devices  46.8 us (13%)
  local copies, waits for them, and re-layouts  16 us (4%)
  other arithmetic  7.53 us (2%)
    all_to_all x2, blocking collectives, exchange(): lax.all_to_all(a, 'ch', split_axis=0, concat_axis=0, axis_index_groups=ri...  163 us
    all_to_all x1, waiting for transfers between devices, per_device(): lax.all_to_all(landed, 'grp', split_axis=0, concat_axis=0, tiled=True)  20.8 us
    pallas_call x1, Pallas kernels, per_device(): pl.pallas_call(functools.partial(mix_kernel, heads, n_z), out_shape=jax.S...  18.6 us
    all_to_all x1, waiting for transfers between devices, per_device(): lax.all_to_all(mixed, 'grp', split_axis=0, concat_axis=0, tiled=True)  18.3 us
    pallas_call x1, Pallas kernels, per_device(): pl.pallas_call(functools.partial(finish_kernel, n_z), out_shape=[jax.Shap...  11.5 us
    pallas_call x1, Pallas kernels, outward(): pl.pallas_call(widen_kernel, out_shape=jax.ShapeDtypeStruct(wide_shape, B...  10.7 us
    ppermute x1, starting transfers between devices, per_device(): got = lax.ppermute(oth, 'ch', swap)  10.5 us
    all_to_all x1, waiting for transfers between devices, exchange(): lax.all_to_all(a, 'ch', split_axis=0, concat_axis=0, axis_index_groups=ri...  10.3 us
  transfers between devices with their start and end apart: 8, of which 4 were waited for; matrix products, arithmetic and copies ran while one was open for 4% of the time, Pallas kernels for 0%

commit v1 on v0

--- a/solution.py
+++ b/solution.py
@@ -7,7 +7,7 @@
 from jax.experimental.pallas import tpu as pltpu
 from jax.sharding import PartitionSpec as P
 
-LEVELS = (96, 128, 144, 152, 160, 168, 176, 184, 192, 200, 208, 224)
+LEVELS = (128, 152, 160, 168, 176, 184, 192, 200, 216)
 LOG2E = 1.4426950408889634
 F32 = jnp.float32
 BF16 = jnp.bfloat16
@@ -113,54 +113,71 @@
     return jnp.dot(pick, rows, preferred_element_type=F32).astype(BF16)
 
 
-def pack_kernel(sc, rows, place, out, pick):
-    @pl.when(pl.program_id(0) == 0)
-    def _():
-        pick[...] = one_hot(out.shape[1], place[0])
-
-    out[0] = chosen(pick[...], rows[...].reshape(place.shape[2], rows.shape[2]))
+def loop(count, body):
+    def step(i, carry):
+        body(i)
+        return carry
+
+    lax.fori_loop(0, count, step, 0, unroll=2)
+
+
+def pack_kernel(sc, rows, place, out):
+    pick = one_hot(out.shape[1], place[sc[0]])
+
+    def body(i):
+        out[i] = chosen(pick, rows[:, i].reshape(place.shape[2], rows.shape[3]))
+
+    loop(out.shape[0], body)
 
 
 def widen_kernel(rows, place, out):
-    one = chosen(one_hot_back(rows.shape[1], place[0]), rows[0])
-    out[0] = one.reshape(out.shape[1:])
+    def body(i):
+        one = chosen(one_hot_back(rows.shape[1], place[i]), rows[i])
+        out[i] = one.reshape(out.shape[1:])
+
+    loop(out.shape[0], body)
 
 
 def order_kernel(count, source, rows, place, out):
-    z = pl.program_id(0)
-    blocks = []
-    for g in range(count):
-        i = source[z * count + g]
-        blocks.append(rows[i // count, i % count])
-    out[0] = chosen(one_hot(out.shape[1], place[0]), jnp.concatenate(blocks, axis=0))
-
-
-def unpack_kernel(sc, rows, place, out, pick):
-    @pl.when(pl.program_id(0) == 0)
-    def _():
-        pick[...] = one_hot_back(rows.shape[1], place[0])
-
-    out[...] = chosen(pick[...], rows[0]).reshape(out.shape)
-
-
-def finish_kernel(spread, sc, rows, own, oth, pick):
+    def body(z):
+        blocks = []
+        for g in range(count):
+            i = source[z * count + g]
+            blocks.append(rows[i // count, i % count])
+        out[z] = chosen(one_hot(out.shape[1], place[z]), jnp.concatenate(blocks, axis=0))
+
+    loop(out.shape[0], body)
+
+
+def unpack_kernel(sc, rows, place, out):
+    pick = one_hot_back(rows.shape[1], place[sc[0]])
+
+    def body(i):
+        one = chosen(pick, rows[i])
+        out[:, i] = one.reshape((out.shape[0],) + out.shape[2:])
+
+    loop(rows.shape[0], body)
+
+
+def finish_kernel(spread, sc, rows, own, oth):
     core, last, filled = sc[0], sc[1], sc[2]
-    length = rows.shape[1]
+    length, width = rows.shape[1:]
     half = length // 2
     keep = length // spread
-
-    @pl.when(pl.program_id(0) == 0)
-    def _():
-        source = lax.broadcasted_iota(jnp.int32, (length, length), 1)
-        index = lax.broadcasted_iota(jnp.int32, (length, length), 0)
-        swapped = jnp.where(index < half, index + half, index - half)
-        t = jnp.minimum(jnp.where(core == 0, index, swapped), last)
-        place = (t % spread) * keep + t // spread
-        pick[...] = jnp.where((source == place) & (filled > 0), 1.0, 0.0).astype(BF16)
-
-    picked = chosen(pick[...], rows[0])
-    own[...] = picked[:half]
-    oth[...] = picked[half:]
+    source = lax.broadcasted_iota(jnp.int32, (length, length), 1)
+    index = lax.broadcasted_iota(jnp.int32, (length, length), 0)
+    swapped = jnp.where(index < half, index + half, index - half)
+    t = jnp.minimum(jnp.where(core == 0, index, swapped), last)
+    place = (t % spread) * keep + t // spread
+    pick = jnp.where((source == place) & (filled > 0), 1.0, 0.0).astype(BF16)
+
+    def body(j):
+        picked = chosen(pick, rows[j])
+        at = pl.ds(pl.multiple_of(j * width, width), width)
+        own[:, at] = picked[:half]
+        oth[:, at] = picked[half:]
+
+    loop(rows.shape[0], body)
 
 
 def norm_kernel(sc, own, oth, gain, out):
@@ -242,17 +259,20 @@
         ],
         axis=0,
     )
-    small_oth = lax.ppermute(small, "ch", swap)
-    shares = jnp.stack(
-        [jnp.where(core == 0, small, small_oth), jnp.where(core == 0, small_oth, small)]
-    )
-
     def exchange(a):
         return lax.all_to_all(
             a, "ch", split_axis=0, concat_axis=0, axis_index_groups=rings, tiled=True
         )
 
-    w_all = exchange(jnp.broadcast_to(shares[None], (n_z, 2, 8, width))).reshape(n_ch, 8, width)
+    by_chip = exchange(jnp.broadcast_to(small[None], (n_z, 8, width)))
+    n_half = n_z // 2
+    w_own = lax.dynamic_slice_in_dim(by_chip, core * n_half, n_half, 0)
+    w_oth = lax.ppermute(
+        lax.dynamic_slice_in_dim(by_chip, other_half * n_half, n_half, 0), "ch", swap
+    )
+    w_mine = jnp.stack(
+        [jnp.where(core == 0, w_own, w_oth), jnp.where(core == 0, w_oth, w_own)], axis=1
+    ).reshape(n_z, 8, width)
 
     pairs = n_grp * n_z
     ids = jnp.arange(pairs, dtype=jnp.int32)
@@ -293,8 +313,7 @@
     step = (
         jax.nn.softplus(dt_both.astype(F32) + bias[None, :]) * valid[:, None].astype(F32)
     ).astype(BF16).astype(F32)
-    rate_all = jnp.exp(w_all[:, 6, ::head_dim])
-    rate = lax.dynamic_slice_in_dim(rate_all, core * chunks, chunks, 0)
+    rate = jnp.exp(w_mine[:, 6, ::head_dim])
 
     def by_chunk(a):
         a = a.reshape(chunks, heads, length)
@@ -315,7 +334,7 @@
                 pl.BlockSpec((half, width), lambda j, sc: (0, j)),
                 whole(bc_in.shape),
                 whole(bc_in.shape),
-                pl.BlockSpec((1, 8, width), lambda j, sc: (sc[0] * chunks + j, 0, 0)),
+                pl.BlockSpec((1, 8, width), lambda j, sc: (j, 0, 0)),
                 whole(wbc.shape),
                 whole(step_t.shape),
                 whole(neg_t.shape),
@@ -330,58 +349,41 @@
             ],
         ),
         name="mix",
-    )(jnp.stack([core, used]).astype(jnp.int32), x_in, x_oth, bc_in, bc_oth, w_all, wbc, step_t, neg_t)
+    )(jnp.stack([core, used]).astype(jnp.int32), x_in, x_oth, bc_in, bc_oth, w_mine, wbc, step_t, neg_t)
 
     spread = lax.all_to_all(mixed, "grp", split_axis=0, concat_axis=0, tiled=True)
 
     full = n_grp * keep
-    my_place = pl.BlockSpec((1, 1, full), lambda i, sc: (sc[0], 0, 0))
-    each_place = pl.BlockSpec((1, 1, full), lambda i, *_: (i, 0, 0))
-    strided = pl.BlockSpec((n_grp, keep, width), lambda i, *_: (0, i, 0))
+    by_pair = (n_grp, n_z, keep, width)
     wide_shape = (n_z, n_grp, keep, width)
 
-    def by_z(size):
-        return pl.BlockSpec((1, size, width), lambda i, *_: (i, 0, 0))
-
-    def short(size):
-        return jax.ShapeDtypeStruct((n_z, size, width), BF16)
+    def once(kernel, scalars, shapes, *operands):
+        many = isinstance(shapes, list)
+        outs = [jax.ShapeDtypeStruct(shape, BF16) for shape in (shapes if many else [shapes])]
+        specs = [whole(out.shape) for out in outs]
+        return pl.pallas_call(
+            kernel,
+            out_shape=outs if many else outs[0],
+            grid_spec=grid_spec(
+                scalars,
+                (1,),
+                [whole(a.shape) for a in operands[scalars:]],
+                specs if many else specs[0],
+            ),
+        )(*operands)
 
     def outward(size, spread):
-        outgoing = pl.pallas_call(
-            pack_kernel,
-            out_shape=short(size),
-            grid_spec=grid_spec(
-                1, (n_z,), [strided, my_place], by_z(size), [pltpu.VMEM((size, full), BF16)]
-            ),
-            name="pack",
-        )(z_only, spread, place_from)
-        return pl.pallas_call(
-            widen_kernel,
-            out_shape=jax.ShapeDtypeStruct(wide_shape, BF16),
-            grid_spec=grid_spec(
-                0,
-                (n_z,),
-                [by_z(size), each_place],
-                pl.BlockSpec((1,) + wide_shape[1:], lambda i: (i, 0, 0, 0)),
-            ),
-            name="widen",
-        )(exchange(outgoing), place_from)
+        outgoing = once(
+            pack_kernel, 1, (n_z, size, width), z_only, spread.reshape(by_pair), place_from
+        )
+        return once(widen_kernel, 0, wide_shape, exchange(outgoing), place_from)
 
     def homeward(size, wide):
-        ordered = pl.pallas_call(
-            functools.partial(order_kernel, n_grp),
-            out_shape=short(size),
-            grid_spec=grid_spec(1, (n_z,), [whole(wide_shape), each_place], by_z(size)),
-            name="order",
-        )(source, wide, place_to)
-        return pl.pallas_call(
-            unpack_kernel,
-            out_shape=jax.ShapeDtypeStruct((n_grp, length, width), BF16),
-            grid_spec=grid_spec(
-                1, (n_z,), [by_z(size), my_place], strided, [pltpu.VMEM((full, size), BF16)]
-            ),
-            name="unpack",
-        )(z_only, exchange(ordered), place_to)
+        ordered = once(
+            functools.partial(order_kernel, n_grp), 1, (n_z, size, width), source, wide, place_to
+        )
+        landed = once(unpack_kernel, 1, by_pair, z_only, exchange(ordered), place_to)
+        return landed.reshape(n_grp, length, width)
 
     sizes = [s for s in LEVELS if s < full] + [full]
 
@@ -397,18 +399,9 @@
     last = jnp.minimum(slot_len[slot] + 3, length - 1)
     filled = jnp.any(target == slot)
     ends_at = jnp.stack([core, last, filled.astype(jnp.int32)]).astype(jnp.int32)
-    own, oth = pl.pallas_call(
-        functools.partial(finish_kernel, n_z),
-        out_shape=[jax.ShapeDtypeStruct((half, mine), BF16)] * 2,
-        grid_spec=grid_spec(
-            1,
-            (chunks,),
-            [pl.BlockSpec((1, length, width), lambda j, sc: (j, 0, 0))],
-            [pl.BlockSpec((half, width), lambda j, sc: (0, j))] * 2,
-            [pltpu.VMEM((length, length), BF16)],
-        ),
-        name="finish",
-    )(ends_at, rows)
+    own, oth = once(
+        functools.partial(finish_kernel, n_z), 1, [(half, mine)] * 2, ends_at, rows
+    )
     got = lax.ppermute(oth, "ch", swap)
     step_rows = 32
     return pl.pallas_call(

time: 361 us -> 326 us (0.903)
  Pallas kernels: 71.9 us -> 46 us
  blocking collectives: 163 us -> 147 us
    pallas_call x5, Pallas kernels: 48.4 us -> 22.5 us  [once(): pl.pallas_call(kernel, out_shape=outs if many else outs[0], grid_spec=gri...]
    all_to_all x2, blocking collectives: 163 us -> 147 us  [exchange(): lax.all_to_all(a, 'ch', split_axis=0, concat_axis=0, axis_index_groups=ri...]
    all_to_all x1, waiting for transfers between devices: 18.3 us -> 26.5 us  [per_device(): lax.all_to_all(mixed, 'grp', split_axis=0, concat_axis=0, tiled=True)]
    ppermute x1, starting transfers between devices: 1.92 us -> 8.71 us  [per_device(): lax.ppermute(lax.dynamic_slice_in_dim(dt_in, other_half * head_half, head...]
    all_to_all x1, waiting for transfers between devices: 10.3 us -> 4.56 us  [exchange(): lax.all_to_all(a, 'ch', split_axis=0, concat_axis=0, axis_index_groups=ri...]
  transfers between devices with their start and end apart: 8 -> 8, of which waited for: 4 -> 5; matrix products, arithmetic and copies ran while one was open for 4% -> 5% of each run, Pallas kernels for 0% -> 0%
where the time goes in v1:
time: 326 us; the launch traced here: 323 us
  blocking collectives  147 us (45%)
  waiting for transfers between devices  55 us (17%)
  starting transfers between devices  49.3 us (15%)
  Pallas kernels  46 us (14%)
  local copies, waits for them, and re-layouts  14.5 us (4%)
  other arithmetic  7.62 us (2%)
    all_to_all x2, blocking collectives, exchange(): lax.all_to_all(a, 'ch', split_axis=0, concat_axis=0, axis_index_groups=ri...  147 us
    all_to_all x1, waiting for transfers between devices, per_device(): lax.all_to_all(mixed, 'grp', split_axis=0, concat_axis=0, tiled=True)  26.5 us
    pallas_call x5, Pallas kernels, once(): pl.pallas_call(kernel, out_shape=outs if many else outs[0], grid_spec=gri...  22.5 us
    all_to_all x1, waiting for transfers between devices, per_device(): lax.all_to_all(landed, 'grp', split_axis=0, concat_axis=0, tiled=True)  20.8 us
    pallas_call x1, Pallas kernels, per_device(): pl.pallas_call(functools.partial(mix_kernel, heads, n_z), out_shape=jax.S...  18.5 us
    ppermute x1, starting transfers between devices, per_device(): got = lax.ppermute(oth, 'ch', swap)  10.5 us
    all_to_all x1, starting transfers between devices, exchange(): lax.all_to_all(a, 'ch', split_axis=0, concat_axis=0, axis_index_groups=ri...  9.61 us
    ppermute x1, starting transfers between devices, per_device(): lax.ppermute(lax.dynamic_slice_in_dim(dt_in, other_half * head_half, head...  8.71 us
  transfers between devices with their start and end apart: 8, of which 5 were waited for; matrix products, arithmetic and copies ran while one was open for 5% of the time, Pallas kernels for 0%

profile of v1, /device:TPU:1, one launch (start us, length us, event | category | flops | bytes accessed | tf_op | source)
XLA Modules:
  0.0 322.7 jit_solution(10559959058642266757)
XLA Ops:
  0.0 0.9 constant_dynamic-slice_fusion.1
  1.0 0.1 copy.148
  1.1 8.7 %collective-permute-start.3 = (bf16[128,64]{0,1:T(8,128)(2,1)S(1)}, bf16[128,64]{0,1:T(8,128)(2,1)S(1)}, u32[]{:S(2)}, u32[]{:S(2)}) collective-permute-start(bf16[128,64]{0,1:T(8,128)(2,1)S(1)} %copy.148), channel_id=1, source_target_pairs={{0,1},{1,0},{2,3},{3,2},{4,5},{5,4},{6,7},{7,6},{8,9},{9,8},{10,11... | collective-permute-start | bytes 49160 | tf_op jit(solution)/shard_map/ppermute | solution.py:249
  9.8 1.9 collective-permute-start.1
  11.7 0.7 broadcast_in_dim.87
  12.4 0.1 broadcast_in_dim_reshape.8
  12.5 0.7 broadcast_in_dim.86
  13.2 0.1 broadcast_in_dim_reshape.7
  13.3 0.7 concatenate.9
  14.0 0.7 broadcast_in_dim.89
  14.7 9.6 %all-to-all-start.20 = ((f32[16,8,256]{2,1,0:T(8,128)}), f32[16,8,256]{2,1,0:T(8,128)S(1)}, u32[]{:S(2)}, u32[]{:S(2)}) async-start(f32[16,8,256]{2,1,0:T(8,128)} %broadcast_in_dim.89), calls=%async_computation.20 | async-start | bytes 262144 | tf_op jit(solution)/shard_map/all_to_all | solution.py:263
  24.3 1.3 constant_dynamic-slice_fusion.3
  25.7 2.7 collective-permute-start
  28.4 0.7 maximum_maximum_fusion.wbc
  29.1 0.6 dynamic_slice.25
  29.7 0.6 compare_convert_fusion
  30.4 1.2 pad_add_fusion.1.sc
  31.6 0.1 copy.147
  31.8 4.6 %all-to-all-done.20 = f32[16,8,256]{2,1,0:T(8,128)S(1)} async-done(((f32[16,8,256]{2,1,0:T(8,128)}), f32[16,8,256]{2,1,0:T(8,128)S(1)}, u32[]{:S(2)}, u32[]{:S(2)}) %all-to-all-start.20) | async-done | bytes 131104 | tf_op jit(solution)/shard_map/all_to_all | solution.py:263
  36.3 5.3 %collective-permute-start.2 = (f32[8,8,256]{2,1,0:T(8,128)S(1)}, f32[8,8,256]{2,1,0:T(8,128)S(1)}, u32[]{:S(2)}, u32[]{:S(2)}) collective-permute-start(f32[8,8,256]{2,1,0:T(8,128)S(1)} %constant_dynamic-slice_fusion.2), channel_id=1, source_target_pairs={{0,1},{1,0},{2,3},{3,2},{4,5},{5,4},{6,7},{7,6},{8,9},{9,8},{10,11... | collective-permute-start | bytes 196616 | tf_op jit(solution)/shard_map/ppermute | solution.py:270
  41.6 0.1 convert_bitcast_fusion
  41.7 0.7 collective-permute-done.2
  42.5 0.1 slice.11
  42.7 0.1 exp.16
  42.8 0.1 negate_multiply_fusion
  42.9 0.7 pad_bitcast_fusion
  43.7 0.6 copy-done.5
  44.3 0.4 copy-done.3
  44.6 18.5 %mix.1 = bf16[16,256,256]{2,1,0:T(8,128)(2,1)} custom-call(s32[2]{0:T(128)} %pad_add_fusion.1.sc, bf16[128,8192]{1,0:T(8,128)(2,1)} %x_own.1, bf16[128,4096]{1,0:T(8,128)(2,1)} %copy-done.3, bf16[128,256]{1,0:T(8,128)(2,1)} %bc_own.1, bf16[128,256]{1,0:T(8,128)(2,1)} %copy-done.5, f32[16,8,256]{2,1,0:T(8,128)} %bitcast.72, ...), custom_call_target="tpu_custom_call" | custom-call | tf_op jit(solution)/shard_map/mix/pallas_call | solution.py:326
  63.2 6.9 %all-to-all-start.21 = ((bf16[16,256,256]{2,1,0:T(8,128)(2,1)}), bf16[16,256,256]{2,1,0:T(8,128)(2,1)S(1)}, u32[]{:S(2)}, u32[]{:S(2)}) async-start(bf16[16,256,256]{2,1,0:T(8,128)(2,1)} %mix.1), calls=%async_computation.21 | async-start | bytes 4194304 | tf_op jit(solution)/shard_map/all_to_all | solution.py:354
  70.2 0.6 compare_reduce_fusion
  70.8 0.2 select_reduce_fusion
  71.4 0.7 slice_reduce_fusion
  72.1 1.9 fusion.8
  75.3 0.1 lt.345
  75.4 0.1 lt.346
  75.6 0.1 add.260
  75.7 0.1 add.261
  75.8 26.5 %all-to-all-done.21 = bf16[16,256,256]{2,1,0:T(8,128)(2,1)S(1)} async-done(((bf16[16,256,256]{2,1,0:T(8,128)(2,1)}), bf16[16,256,256]{2,1,0:T(8,128)(2,1)S(1)}, u32[]{:S(2)}, u32[]{:S(2)}) %all-to-all-start.21) | async-done | bytes 2097184 | tf_op jit(solution)/shard_map/all_to_all | solution.py:354
  102.3 76.0 %conditional.2 = (bf16[16,16,16,256]{3,2,1,0:T(8,128)(2,1)S(1)}) conditional(s32[]{:T(128)} %clamp.7, (bf16[16,256,256]{2,1,0:T(8,128)(2,1)S(1)}, s32[1]{0:T(128)}, s32[16,1,256]{2,1,0:T(1,128)S(1)}) %tuple.77, (bf16[16,256,256]{2,1,0:T(8,128)(2,1)S(1)}, s32[1]{0:T(128)}, s32[16,1,256]{2,1,0:T(1,128)S(1)}) %tuple.77, ...), branch_computations={%region_10.11_spmd, %region_11.12_spmd, %region_12.13_spmd, %regio... | conditional | bytes 4194312 | solution.py:392
  102.3 2.8 branch_4_fun.4
  105.1 68.3 %all_to_all.99.rows = bf16[16,176,256]{2,1,0:T(8,128)(2,1)} all-to-all(bf16[16,176,256]{2,1,0:T(8,128)(2,1)} %branch_4_fun.4), channel_id=1, replica_groups={{0,2,4,6,8,10,12,14,16,18,20,22,24,26,28,30},{1,3,5,7,9,11,13,15,17,19,..., dimensions={0} | all-to-all | bytes 2883584 | tf_op jit(solution)/shard_map/cond/branch_4_fun/all_to_all | solution.py:263
  173.4 4.9 %branch_4_fun.5 = bf16[16,16,16,256]{3,2,1,0:T(8,128)(2,1)S(1)} custom-call(bf16[16,176,256]{2,1,0:T(8,128)(2,1)} %all_to_all.99.rows, s32[16,1,256]{2,1,0:T(1,128)S(1)} %get-tuple-element.352.place), custom_call_target="tpu_custom_call" | custom-call | tf_op jit(solution)/shard_map/cond/branch_4_fun/pallas_call | solution.py:364
  178.3 90.3 %conditional.3 = (bf16[16,16,16,256]{3,2,1,0:T(8,128)(2,1)S(1)}) conditional(s32[]{:T(128)} %clamp.6, (s32[16,16]{0,1:T(8,128)S(1)}, s32[256]{0:T(256)S(1)}, s32[256]{0:T(256)S(1)}, s32[16,16]{0,1:T(8,128)S(1)}, s32[16,16]{0,1:T(8,128)S(1)}, /*index=5*/s32[16,1,256]{2,1,0:T(1,128)S(1)}, ...), branch_computations={%region_20.21_spmd, %region_21.22_spmd, %region_22.23_spmd, %regio... | conditional | flops 12288 | bytes 4370440 | solution.py:392
  178.8 0.6 reshape.654.source
  179.4 0.1 lt.254
  179.5 0.1 lt.255
  179.6 0.1 add.207
  179.7 0.1 add.208
  179.8 0.6 compare_select_fusion.6.place
  180.5 5.7 %branch_6_fun.6 = bf16[16,192,256]{2,1,0:T(8,128)(2,1)} custom-call(s32[256]{0:T(256)} %reshape.654.source, bf16[16,16,16,256]{3,2,1,0:T(8,128)(2,1)S(1)} %get-tuple-element.418.rows, s32[16,1,256]{2,1,0:T(1,128)} %compare_select_fusion.6.place), custom_call_target="tpu_custom_call" | custom-call | tf_op jit(solution)/shard_map/cond/branch_6_fun/pallas_call | solution.py:364
  186.2 78.9 %all_to_all.111.rows = bf16[16,192,256]{2,1,0:T(8,128)(2,1)} all-to-all(bf16[16,192,256]{2,1,0:T(8,128)(2,1)} %branch_6_fun.6), channel_id=1, replica_groups={{0,2,4,6,8,10,12,14,16,18,20,22,24,26,28,30},{1,3,5,7,9,11,13,15,17,19,..., dimensions={0} | all-to-all | bytes 3145728 | tf_op jit(solution)/shard_map/cond/branch_6_fun/all_to_all | solution.py:263
  265.1 3.4 %branch_6_fun.7 = bf16[16,16,16,256]{3,2,1,0:T(8,128)(2,1)S(1)} custom-call(s32[1]{0:T(128)} %get-tuple-element.416.sc, bf16[16,192,256]{2,1,0:T(8,128)(2,1)} %all_to_all.111.rows, s32[16,1,256]{2,1,0:T(1,128)} %compare_select_fusion.6.place), custom_call_target="tpu_custom_call" | custom-call | tf_op jit(solution)/shard_map/cond/branch_6_fun/pallas_call | solution.py:364
  268.6 1.3 copy-done.1
  269.9 3.7 %all-to-all-start.22 = ((bf16[16,256,256]{2,1,0:T(8,128)(2,1)}), bf16[16,256,256]{2,1,0:T(8,128)(2,1)S(1)}, u32[]{:S(2)}, u32[]{:S(2)}) async-start(bf16[16,256,256]{2,1,0:T(8,128)(2,1)} %bitcast.50), calls=%async_computation.22 | async-start | bytes 4194304 | tf_op jit(solution)/shard_map/all_to_all | solution.py:396
  274.3 0.6 dynamic_slice.24
  275.4 0.6 pad_add_fusion.sc
  276.0 20.8 %all-to-all-done.22.rows = bf16[16,256,256]{2,1,0:T(8,128)(2,1)S(1)} async-done(((bf16[16,256,256]{2,1,0:T(8,128)(2,1)}), bf16[16,256,256]{2,1,0:T(8,128)(2,1)S(1)}, u32[]{:S(2)}, u32[]{:S(2)}) %all-to-all-start.22) | async-done | bytes 2097184 | tf_op jit(solution)/shard_map/all_to_all | solution.py:396
  296.8 1.3 copy-done
  298.1 5.6 %shard_map.154 = (bf16[128,4096]{1,0:T(8,128)(2,1)}, bf16[128,4096]{1,0:T(8,128)(2,1)}) custom-call(s32[3]{0:T(128)} %pad_add_fusion.sc, bf16[16,256,256]{2,1,0:T(8,128)(2,1)} %copy-done), custom_call_target="tpu_custom_call" | custom-call | tf_op jit(solution)/shard_map/pallas_call | solution.py:364
  303.7 10.5 %collective-permute-start.4 = (bf16[128,4096]{1,0:T(8,128)(2,1)}, bf16[128,4096]{1,0:T(8,128)(2,1)S(1)}, u32[]{:S(2)}, u32[]{:S(2)}) collective-permute-start(bf16[128,4096]{1,0:T(8,128)(2,1)} %get-tuple-element.451), channel_id=1, source_target_pairs={{0,1},{1,0},{2,3},{3,2},{4,5},{5,4},{6,7},{7,6},{8,9},{9,8},{10,11... | collective-permute-start | bytes 3145736 | tf_op jit(solution)/shard_map/ppermute | solution.py:405
  314.2 2.5 collective-permute-done.4.oth
  316.7 1.0 copy-done.2
  317.7 5.0 %norm.1 = bf16[128,8192]{1,0:T(8,128)(2,1)} custom-call(s32[3]{0:T(128)} %pad_add_fusion.sc, bf16[128,4096]{1,0:T(8,128)(2,1)} %get-tuple-element.450.own, bf16[128,4096]{1,0:T(8,128)(2,1)} %copy-done.2, f32[1,8192]{1,0:T(1,128)} %bitcast.74), custom_call_target="tpu_custom_call" | custom-call | tf_op jit(solution)/shard_map/norm/pallas_call | solution.py:407
  (53 shorter events, 1.1 us)
Async XLA Ops:
  0.0 28.4 %copy-start.9 = (f32[256]{0:T(256)S(1)}, f32[256]{0:T(256)}, u32[]{:S(2)}) copy-start(f32[256]{0:T(256)} %param.45) | copy-start | bytes 3076
  0.0 28.4 %copy-start.6 = (f32[4,256]{1,0:T(4,128)S(1)}, f32[4,256]{1,0:T(4,128)}, u32[]{:S(2)}) copy-start(f32[4,256]{1,0:T(4,128)} %param.44) | copy-start | bytes 12292
  0.0 29.1 %copy-start.7 = (s32[256]{0:T(256)S(1)}, s32[256]{0:T(256)}, u32[]{:S(2)}) copy-start(s32[256]{0:T(256)} %param.47) | copy-start | bytes 3076
  0.0 31.6 %copy-start.12 = (f32[128]{0:T(128)S(1)}, f32[128]{0:T(128)}, u32[]{:S(2)}) copy-start(f32[128]{0:T(128)} %param.39) | copy-start | bytes 1540
  1.1 30.7 %collective-permute-start.3 = (bf16[128,64]{0,1:T(8,128)(2,1)S(1)}, bf16[128,64]{0,1:T(8,128)(2,1)S(1)}, u32[]{:S(2)}, u32[]{:S(2)}) collective-permute-start(bf16[128,64]{0,1:T(8,128)(2,1)S(1)} %copy.148), channel_id=1, source_target_pairs={{0,1},{1,0},{2,3},{3,2},{4,5},{5,4},{6,7},{7,6},{8,9},{9,8},{10,11... | collective-permute-start | bytes 49160 | tf_op jit(solution)/shard_map/ppermute | solution.py:249
  9.8 33.8 %collective-permute-start.1 = (bf16[128,256]{1,0:T(8,128)(2,1)}, bf16[128,256]{1,0:T(8,128)(2,1)S(1)}, u32[]{:S(2)}, u32[]{:S(2)}) collective-permute-start(bf16[128,256]{1,0:T(8,128)(2,1)} %bc_own.1), channel_id=1, source_target_pairs={{0,1},{1,0},{2,3},{3,2},{4,5},{5,4},{6,7},{7,6},{8,9},{9,8},{10,11... | collective-permute-start | bytes 196616 | tf_op jit(solution)/shard_map/ppermute | solution.py:248
  14.7 21.6 %all-to-all-start.20 = ((f32[16,8,256]{2,1,0:T(8,128)}), f32[16,8,256]{2,1,0:T(8,128)S(1)}, u32[]{:S(2)}, u32[]{:S(2)}) async-start(f32[16,8,256]{2,1,0:T(8,128)} %broadcast_in_dim.89), calls=%async_computation.20 | async-start | bytes 262144 | tf_op jit(solution)/shard_map/all_to_all | solution.py:263
  25.7 18.0 %collective-permute-start = (bf16[128,4096]{1,0:T(8,128)(2,1)S(1)}, bf16[128,4096]{1,0:T(8,128)(2,1)S(1)}, u32[]{:S(2)}, u32[]{:S(2)}) collective-permute-start(bf16[128,4096]{1,0:T(8,128)(2,1)S(1)} %constant_dynamic-slice_fusion.3), channel_id=1, source_target_pairs={{0,1},{1,0},{2,3},{3,2},{4,5},{5,4},{6,7},{7,6},{8,9},{9,8},{10,11... | collective-permute-start | bytes 3145736 | tf_op jit(solution)/shard_map/ppermute | solution.py:245
  36.3 6.1 %collective-permute-start.2 = (f32[8,8,256]{2,1,0:T(8,128)S(1)}, f32[8,8,256]{2,1,0:T(8,128)S(1)}, u32[]{:S(2)}, u32[]{:S(2)}) collective-permute-start(f32[8,8,256]{2,1,0:T(8,128)S(1)} %constant_dynamic-slice_fusion.2), channel_id=1, source_target_pairs={{0,1},{1,0},{2,3},{3,2},{4,5},{5,4},{6,7},{7,6},{8,9},{9,8},{10,11... | collective-permute-start | bytes 196616 | tf_op jit(solution)/shard_map/ppermute | solution.py:270
  42.5 1.1 copy-start.4
  43.6 0.6 copy-start.5
  43.6 1.0 copy-start.3
  63.1 6.9 %copy-start.8 = (s32[256]{0:T(256)S(1)}, s32[256]{0:T(256)}, u32[]{:S(2)}) copy-start(s32[256]{0:T(256)} %param.48) | copy-start | bytes 3076
  63.1 7.0 %copy-start.10 = (s32[256]{0:T(256)S(1)}, s32[256]{0:T(256)}, u32[]{:S(2)}) copy-start(s32[256]{0:T(256)} %param.49) | copy-start | bytes 3076
  63.1 8.9 %copy-start.11 = (s32[9]{0:T(128)S(1)}, s32[9]{0:T(128)}, u32[]{:S(2)}) copy-start(s32[9]{0:T(128)} %constant.114.clone) | copy-start | bytes 112
  63.2 39.1 %all-to-all-start.21 = ((bf16[16,256,256]{2,1,0:T(8,128)(2,1)}), bf16[16,256,256]{2,1,0:T(8,128)(2,1)S(1)}, u32[]{:S(2)}, u32[]{:S(2)}) async-start(bf16[16,256,256]{2,1,0:T(8,128)(2,1)} %mix.1), calls=%async_computation.21 | async-start | bytes 4194304 | tf_op jit(solution)/shard_map/all_to_all | solution.py:354
  268.6 1.3 copy-start.1
  269.9 26.9 %all-to-all-start.22 = ((bf16[16,256,256]{2,1,0:T(8,128)(2,1)}), bf16[16,256,256]{2,1,0:T(8,128)(2,1)S(1)}, u32[]{:S(2)}, u32[]{:S(2)}) async-start(bf16[16,256,256]{2,1,0:T(8,128)(2,1)} %bitcast.50), calls=%async_computation.22 | async-start | bytes 4194304 | tf_op jit(solution)/shard_map/all_to_all | solution.py:396
  296.8 1.3 copy-start
  303.7 13.0 %collective-permute-start.4 = (bf16[128,4096]{1,0:T(8,128)(2,1)}, bf16[128,4096]{1,0:T(8,128)(2,1)S(1)}, u32[]{:S(2)}, u32[]{:S(2)}) collective-permute-start(bf16[128,4096]{1,0:T(8,128)(2,1)} %get-tuple-element.451), channel_id=1, source_target_pairs={{0,1},{1,0},{2,3},{3,2},{4,5},{5,4},{6,7},{7,6},{8,9},{9,8},{10,11... | collective-permute-start | bytes 3145736 | tf_op jit(solution)/shard_map/ppermute | solution.py:405
  316.7 1.0 copy-start.2

commit v2 on v1

--- a/solution.py
+++ b/solution.py
@@ -26,52 +26,74 @@
     return low + low * jnp.tanh(low)
 
 
+def small_kernel(skip, rate, taps, bias, out):
+    count, width = out.shape[0], out.shape[2]
+    heads = skip.shape[0]
+    lane = lax.broadcasted_iota(jnp.int32, (1, width), 1)
+
+    def by_channel(values):
+        spread = jnp.full((1, width), values[0], F32)
+        for h in range(1, heads):
+            spread = jnp.where(lane >= h * (width // heads), values[h], spread)
+        return spread
+
+    rows = [taps[...], bias[...], by_channel(skip), by_channel(rate), jnp.zeros((1, width), F32)]
+    share = jnp.concatenate(rows, axis=0)
+    for i in range(count):
+        out[i] = share
+
+
+def joined(core, used, own, oth, buffer):
+    buffer[core] = own
+    buffer[1 - core] = oth
+    both = buffer[...].reshape(2 * own.shape[0], own.shape[1]).astype(F32)
+    rows = lax.broadcasted_iota(jnp.int32, both.shape, 0)
+    return jnp.where(rows < used, both, 0.0), rows
+
+
+def prep_kernel(spread, sc, bc_own, bc_oth, wbc, step, scores, summed, pick, buffer):
+    bc, rows = joined(sc[0], sc[1], bc_own[...], bc_oth[...], buffer)
+    length = bc.shape[0]
+    act = conv_silu(bc, wbc[0:4], wbc[4:5], rows)
+    state = act.shape[1] // 2
+    later = lax.broadcasted_iota(jnp.int32, (length, length), 0)
+    earlier = lax.broadcasted_iota(jnp.int32, (length, length), 1)
+    raw = lax.dot_general(
+        act[:, state:],
+        act[:, :state],
+        (((1,), (1,)), ((), ())),
+        precision=lax.Precision.HIGHEST,
+        preferred_element_type=F32,
+    )
+    scores[...] = jnp.where(later >= earlier, raw, 0.0)
+    upper = jnp.where(later <= earlier, 1.0, 0.0).astype(F32)
+    summed[...] = LOG2E * jnp.dot(
+        step[...], upper, precision=lax.Precision.HIGHEST, preferred_element_type=F32
+    )
+    keep = length // spread
+    place = (later % keep) * spread + later // keep
+    pick[...] = jnp.where(earlier == place, 1.0, 0.0).astype(BF16)
+
+
 def mix_kernel(
-    heads, spread, sc, x_own, x_oth, bc_own, bc_oth, w, wbc, step, neg, out,
-    scores, decay, pick, joint, joint_bc,
+    heads, sc, x_own, x_oth, w_own, w_oth, step, scores, summed, pick, out, joint
 ):
     core, used = sc[0], sc[1]
     j = pl.program_id(0)
     half, width = x_own.shape
     length = 2 * half
-
-    def joined(own, oth, buffer):
-        buffer[core] = own[...]
-        buffer[1 - core] = oth[...]
-        both = buffer[...].reshape(length, own.shape[1]).astype(F32)
-        rows = lax.broadcasted_iota(jnp.int32, both.shape, 0)
-        return jnp.where(rows < used, both, 0.0), rows
-
-    @pl.when(j == 0)
-    def _():
-        bc, rows = joined(bc_own, bc_oth, joint_bc)
-        act = conv_silu(bc, wbc[0:4], wbc[4:5], rows)
-        state = act.shape[1] // 2
-        later = lax.broadcasted_iota(jnp.int32, (length, length), 0)
-        earlier = lax.broadcasted_iota(jnp.int32, (length, length), 1)
-        raw = lax.dot_general(
-            act[:, state:],
-            act[:, :state],
-            (((1,), (1,)), ((), ())),
-            precision=lax.Precision.HIGHEST,
-            preferred_element_type=F32,
-        )
-        scores[...] = jnp.where(later >= earlier, raw, 0.0)
-        upper = jnp.where(later <= earlier, 1.0, 0.0).astype(F32)
-        decay[...] = LOG2E * jnp.dot(
-            neg[...], upper, precision=lax.Precision.HIGHEST, preferred_element_type=F32
-        )
-        keep = length // spread
-        place = (later % keep) * spread + later // keep
-        pick[...] = jnp.where(earlier == place, 1.0, 0.0).astype(BF16)
-
-    x, rows = joined(x_own, x_oth, joint)
-    x_act = conv_silu(x, w[0, 0:4], w[0, 4:5], rows)
+    columns = pl.ds(pl.multiple_of(j * width, width), width)
+    x, rows = joined(core, used, x_own[...], x_oth[:, columns], joint)
+    w = jnp.where(j % 2 == core, w_own[j // 2], w_oth[j // 2])
+    x_act = conv_silu(x, w[0:4], w[4:5], rows)
     at = pl.ds(pl.multiple_of(8 * j, 8), 8)
-    decay_rows = decay[at]
+    dim = width // heads
+    rates = -jnp.exp(w[6:7])
+    sums_here = summed[at]
+    scaled = [sums_here[h : h + 1] * rates[:, h * dim : h * dim + 1] for h in range(heads)]
+    decay_rows = jnp.concatenate(scaled + [sums_here[heads:]], axis=0)
     decay_cols = jnp.transpose(decay_rows)
     step_cols = jnp.transpose(step[at])
-    dim = width // heads
     pair = 2 * dim
     first = lax.broadcasted_iota(jnp.int32, (length, pair), 1) < dim
     mixed = []
@@ -93,7 +115,7 @@
                 parts.append(both[:, :pair] + both[:, pair:])
             sums.append(jnp.concatenate(parts, axis=0))
         mixed.append(jnp.where(first, sums[0], sums[1]))
-    result = jnp.concatenate(mixed, axis=1) + w[0, 5:6] * x_act
+    result = jnp.concatenate(mixed, axis=1) + w[5:6] * x_act
     out[0] = jnp.dot(pick[...], result.astype(BF16), preferred_element_type=F32).astype(BF16)
 
 
@@ -183,7 +205,9 @@
 def norm_kernel(sc, own, oth, gain, out):
     core = sc[0]
     width = own.shape[1]
-    mine, other = own[...].astype(F32), oth[...].astype(F32)
+    count = out.shape[0]
+    here = pl.ds(pl.multiple_of(pl.program_id(0) * count, count), count)
+    mine, other = own[here].astype(F32), oth[here].astype(F32)
     total = jnp.sum(mine * mine, axis=1, keepdims=True) + jnp.sum(
         other * other, axis=1, keepdims=True
     )
@@ -203,8 +227,19 @@
     )
 
 
-def whole(shape):
-    return pl.BlockSpec(shape, lambda *_: (0,) * len(shape))
+def resident():
+    return pl.BlockSpec(memory_space=pltpu.VMEM)
+
+
+def once(kernel, scalars, outs, *operands, scratch=()):
+    return pl.pallas_call(
+        kernel,
+        out_shape=outs,
+        in_specs=[pl.BlockSpec(memory_space=pltpu.SMEM)] * scalars
+        + [resident()] * (len(operands) - scalars),
+        out_specs=jax.tree.map(lambda _: resident(), outs),
+        scratch_shapes=list(scratch),
+    )(*operands)
 
 
 def per_device(
@@ -249,31 +284,22 @@
     dt_oth = lax.ppermute(
         lax.dynamic_slice_in_dim(dt_in, other_half * head_half, head_half, 1), "ch", swap
     )
-    small = jnp.concatenate(
-        [
-            conv_x,
-            conv_x_bias[None],
-            jnp.repeat(skip_d, head_dim)[None],
-            jnp.repeat(a_log, head_dim)[None],
-            jnp.zeros((1, width), F32),
-        ],
-        axis=0,
-    )
+    shares = once(
+        small_kernel,
+        2,
+        jax.ShapeDtypeStruct((n_z, 8, width), F32),
+        skip_d,
+        a_log,
+        conv_x,
+        conv_x_bias[None],
+    )
+
     def exchange(a):
         return lax.all_to_all(
             a, "ch", split_axis=0, concat_axis=0, axis_index_groups=rings, tiled=True
         )
 
-    by_chip = exchange(jnp.broadcast_to(small[None], (n_z, 8, width)))
-    n_half = n_z // 2
-    w_own = lax.dynamic_slice_in_dim(by_chip, core * n_half, n_half, 0)
-    w_oth = lax.ppermute(
-        lax.dynamic_slice_in_dim(by_chip, other_half * n_half, n_half, 0), "ch", swap
-    )
-    w_mine = jnp.stack(
-        [jnp.where(core == 0, w_own, w_oth), jnp.where(core == 0, w_oth, w_own)], axis=1
-    ).reshape(n_z, 8, width)
-
+    by_chip = exchange(shares)
     pairs = n_grp * n_z
     ids = jnp.arange(pairs, dtype=jnp.int32)
     alive = dest_group >= 0
@@ -301,6 +327,7 @@
     place_from = places(by_group, starts)
     place_to = places(to_units, to_starts)
     source = source.reshape(n_grp, n_z).T.reshape(-1)
+    place_from, place_to, source = lax.optimization_barrier((place_from, place_to, source))
     z_only = my_z[None].astype(jnp.int32)
 
     my_dt = lax.dynamic_slice_in_dim(dt_in, core * head_half, head_half, 1)
@@ -313,43 +340,49 @@
     step = (
         jax.nn.softplus(dt_both.astype(F32) + bias[None, :]) * valid[:, None].astype(F32)
     ).astype(BF16).astype(F32)
-    rate = jnp.exp(w_mine[:, 6, ::head_dim])
 
     def by_chunk(a):
         a = a.reshape(chunks, heads, length)
         return jnp.pad(a, ((0, 0), (0, 8 - heads), (0, 0))).reshape(chunks * 8, length)
 
     step_t = by_chunk(step.T)
-    neg_t = by_chunk(-step.T * rate.reshape(-1)[:, None])
     wbc = jnp.concatenate([conv_bc, conv_bc_bias[None], jnp.zeros((3, conv_bc.shape[1]), F32)], axis=0)
 
+    where_am_i = jnp.stack([core, used]).astype(jnp.int32)
+    scores, summed, pick = once(
+        functools.partial(prep_kernel, n_z),
+        1,
+        [
+            jax.ShapeDtypeStruct((length, length), F32),
+            jax.ShapeDtypeStruct(step_t.shape, F32),
+            jax.ShapeDtypeStruct((length, length), BF16),
+        ],
+        where_am_i,
+        bc_in,
+        bc_oth,
+        wbc,
+        step_t,
+        scratch=[pltpu.VMEM((2,) + bc_in.shape, BF16)],
+    )
+    by_chip, scores = lax.optimization_barrier((by_chip, scores))
+    n_half = n_z // 2
+    w_own = lax.dynamic_slice_in_dim(by_chip, core * n_half, n_half, 0)
+    w_oth = lax.ppermute(
+        lax.dynamic_slice_in_dim(by_chip, other_half * n_half, n_half, 0), "ch", swap
+    )
     mixed = pl.pallas_call(
-        functools.partial(mix_kernel, heads, n_z),
+        functools.partial(mix_kernel, heads),
         out_shape=jax.ShapeDtypeStruct((chunks, length, width), BF16),
         grid_spec=grid_spec(
             1,
             (chunks,),
-            [
-                pl.BlockSpec((half, width), lambda j, sc: (0, sc[0] * chunks + j)),
-                pl.BlockSpec((half, width), lambda j, sc: (0, j)),
-                whole(bc_in.shape),
-                whole(bc_in.shape),
-                pl.BlockSpec((1, 8, width), lambda j, sc: (j, 0, 0)),
-                whole(wbc.shape),
-                whole(step_t.shape),
-                whole(neg_t.shape),
-            ],
+            [pl.BlockSpec((half, width), lambda j, sc: (0, sc[0] * chunks + j))]
+            + [resident()] * 7,
             pl.BlockSpec((1, length, width), lambda j, sc: (j, 0, 0)),
-            [
-                pltpu.VMEM((length, length), F32),
-                pltpu.VMEM((chunks * 8, length), F32),
-                pltpu.VMEM((length, length), BF16),
-                pltpu.VMEM((2, half, width), BF16),
-                pltpu.VMEM((2,) + bc_in.shape, BF16),
-            ],
+            [pltpu.VMEM((2, half, width), BF16)],
         ),
         name="mix",
-    )(jnp.stack([core, used]).astype(jnp.int32), x_in, x_oth, bc_in, bc_oth, w_mine, wbc, step_t, neg_t)
+    )(where_am_i, x_in, x_oth, w_own, w_oth, step_t, scores, summed, pick)
 
     spread = lax.all_to_all(mixed, "grp", split_axis=0, concat_axis=0, tiled=True)
 
@@ -357,32 +390,20 @@
     by_pair = (n_grp, n_z, keep, width)
     wide_shape = (n_z, n_grp, keep, width)
 
-    def once(kernel, scalars, shapes, *operands):
-        many = isinstance(shapes, list)
-        outs = [jax.ShapeDtypeStruct(shape, BF16) for shape in (shapes if many else [shapes])]
-        specs = [whole(out.shape) for out in outs]
-        return pl.pallas_call(
-            kernel,
-            out_shape=outs if many else outs[0],
-            grid_spec=grid_spec(
-                scalars,
-                (1,),
-                [whole(a.shape) for a in operands[scalars:]],
-                specs if many else specs[0],
-            ),
-        )(*operands)
+    def bf16(*shape):
+        return jax.ShapeDtypeStruct(shape, BF16)
 
     def outward(size, spread):
         outgoing = once(
-            pack_kernel, 1, (n_z, size, width), z_only, spread.reshape(by_pair), place_from
+            pack_kernel, 1, bf16(n_z, size, width), z_only, spread.reshape(by_pair), place_from
         )
-        return once(widen_kernel, 0, wide_shape, exchange(outgoing), place_from)
+        return once(widen_kernel, 0, bf16(*wide_shape), exchange(outgoing), place_from)
 
     def homeward(size, wide):
         ordered = once(
-            functools.partial(order_kernel, n_grp), 1, (n_z, size, width), source, wide, place_to
+            functools.partial(order_kernel, n_grp), 1, bf16(n_z, size, width), source, wide, place_to
         )
-        landed = once(unpack_kernel, 1, by_pair, z_only, exchange(ordered), place_to)
+        landed = once(unpack_kernel, 1, bf16(*by_pair), z_only, exchange(ordered), place_to)
         return landed.reshape(n_grp, length, width)
 
     sizes = [s for s in LEVELS if s < full] + [full]
@@ -400,7 +421,7 @@
     filled = jnp.any(target == slot)
     ends_at = jnp.stack([core, last, filled.astype(jnp.int32)]).astype(jnp.int32)
     own, oth = once(
-        functools.partial(finish_kernel, n_z), 1, [(half, mine)] * 2, ends_at, rows
+        functools.partial(finish_kernel, n_z), 1, [bf16(half, mine)] * 2, ends_at, rows
     )
     got = lax.ppermute(oth, "ch", swap)
     step_rows = 32
@@ -410,7 +431,7 @@
         grid_spec=grid_spec(
             1,
             (half // step_rows,),
-            [pl.BlockSpec((step_rows, mine), lambda i, sc: (i, 0))] * 2 + [whole((1, channels))],
+            [resident()] * 3,
             pl.BlockSpec((step_rows, channels), lambda i, sc: (i, 0)),
         ),
         name="norm",

time: 326 us -> 324 us (level)
  waiting for transfers between devices: 55 us -> 49.6 us
  local copies, waits for them, and re-layouts: 14.5 us -> 11.2 us
    all_to_all x1, waiting for transfers between devices: 4.56 us -> 0.3 us  [exchange(): lax.all_to_all(a, 'ch', split_axis=0, concat_axis=0, axis_index_groups=ri...]
    pallas_call x6 -> x8, Pallas kernels: 41 us -> 43.8 us  [the longest x7 24.8 us: once(): pl.pallas_call(kernel, out_shape=outs, in_specs=[pl.BlockSpec(memory_spac...]
  transfers between devices with their start and end apart: 8 -> 8, of which waited for: 5 -> 5; matrix products, arithmetic and copies ran while one was open for 5% -> 4% of each run, Pallas kernels for 0% -> 1%
where the time goes in v2:
time: 324 us; the launch traced here: 319 us
  blocking collectives  149 us (46%)
  waiting for transfers between devices  49.6 us (15%)
  starting transfers between devices  49.3 us (15%)
  Pallas kernels  48.5 us (15%)
  local copies, waits for them, and re-layouts  11.2 us (3%)
  other arithmetic  7.91 us (2%)
    all_to_all x2, blocking collectives, exchange(): lax.all_to_all(a, 'ch', split_axis=0, concat_axis=0, axis_index_groups=ri...  149 us
    all_to_all x1, waiting for transfers between devices, per_device(): lax.all_to_all(mixed, 'grp', split_axis=0, concat_axis=0, tiled=True)  25.5 us
    pallas_call x7, Pallas kernels, once(): pl.pallas_call(kernel, out_shape=outs, in_specs=[pl.BlockSpec(memory_spac...  24.8 us
    all_to_all x1, waiting for transfers between devices, per_device(): lax.all_to_all(landed, 'grp', split_axis=0, concat_axis=0, tiled=True)  20.5 us
    pallas_call x1, Pallas kernels, per_device(): pl.pallas_call(functools.partial(mix_kernel, heads), out_shape=jax.ShapeD...  19 us
    ppermute x1, starting transfers between devices, per_device(): got = lax.ppermute(oth, 'ch', swap)  10.5 us
    all_to_all x1, starting transfers between devices, exchange(): lax.all_to_all(a, 'ch', split_axis=0, concat_axis=0, axis_index_groups=ri...  9.57 us
    ppermute x1, starting transfers between devices, per_device(): lax.ppermute(lax.dynamic_slice_in_dim(dt_in, other_half * head_half, head...  8.74 us
  transfers between devices with their start and end apart: 8, of which 5 were waited for; matrix products, arithmetic and copies ran while one was open for 4% of the time, Pallas kernels for 1%

profile of v2, /device:TPU:1, one launch (start us, length us, event | category | flops | bytes accessed | tf_op | source)
XLA Modules:
  0.0 319.2 jit_solution(4211923804078747853)
XLA Ops:
  0.1 0.9 constant_dynamic-slice_fusion.2
  0.9 8.7 %collective-permute-start.2 = (bf16[128,64]{1,0:T(8,128)(2,1)S(1)}, bf16[128,64]{1,0:T(8,128)(2,1)S(1)}, u32[]{:S(2)}, u32[]{:S(2)}) collective-permute-start(bf16[128,64]{1,0:T(8,128)(2,1)S(1)} %constant_dynamic-slice_fusion.2), channel_id=1, source_target_pairs={{0,1},{1,0},{2,3},{3,2},{4,5},{5,4},{6,7},{7,6},{8,9},{9,8},{10,11... | collective-permute-start | bytes 49160 | tf_op jit(solution)/shard_map/ppermute | solution.py:284
  9.7 1.9 collective-permute-start.1
  11.6 1.4 shard_map.154
  13.0 9.6 %all-to-all-start.20 = ((f32[16,8,256]{2,1,0:T(8,128)}), f32[16,8,256]{2,1,0:T(8,128)S(1)}, u32[]{:S(2)}, u32[]{:S(2)}) async-start(f32[16,8,256]{2,1,0:T(8,128)} %shard_map.154), calls=%async_computation.20 | async-start | bytes 262144 | tf_op jit(solution)/shard_map/all_to_all | solution.py:298
  22.6 1.3 constant_dynamic-slice_fusion.3
  23.9 2.7 collective-permute-start
  26.6 0.7 dynamic_slice.25
  27.2 0.7 compare_convert_fusion
  27.9 0.1 pad.10.clone
  28.0 0.7 maximum_maximum_fusion.wbc
  28.7 1.3 pad_add_fusion.1.sc
  30.0 0.1 dynamic_slice.29
  30.1 0.1 broadcast_select_fusion.1
  30.2 0.1 fusion.2
  30.3 0.1 copy.38
  30.4 0.7 bitcast_convert_fusion.step
  31.1 0.6 copy-done.6
  31.7 2.5 shard_map.155
  34.2 0.3 all-to-all-done.20
  34.5 0.6 constant_dynamic-slice_fusion
  35.2 5.3 %collective-permute-start.3 = (f32[8,8,256]{2,1,0:T(8,128)S(1)}, f32[8,8,256]{2,1,0:T(8,128)S(1)}, u32[]{:S(2)}, u32[]{:S(2)}) collective-permute-start(f32[8,8,256]{2,1,0:T(8,128)S(1)} %get-tuple-element.265), channel_id=1, source_target_pairs={{0,1},{1,0},{2,3},{3,2},{4,5},{5,4},{6,7},{7,6},{8,9},{9,8},{10,11... | collective-permute-start | bytes 196616 | tf_op jit(solution)/shard_map/ppermute | solution.py:370
  40.4 0.9 collective-permute-done.3.w_oth
  41.3 0.6 copy-done.5
  41.9 0.4 copy-done.3
  42.3 19.0 %mix.1 = bf16[16,256,256]{2,1,0:T(8,128)(2,1)} custom-call(s32[2]{0:T(128)} %pad_add_fusion.1.sc, bf16[128,8192]{1,0:T(8,128)(2,1)} %x_own.1, bf16[128,4096]{1,0:T(8,128)(2,1)} %copy-done.3, f32[8,8,256]{2,1,0:T(8,128)} %get-tuple-element.266.w_own, f32[8,8,256]{2,1,0:T(8,128)} %copy-done.5, f32[128,256]{1,0:T(8,128)} %bitcast_convert_fusion.step, ...), custom_call_target="tpu_custom_call" | custom-call | tf_op jit(solution)/shard_map/mix/pallas_call | solution.py:373
  61.3 6.9 %all-to-all-start.21 = ((bf16[16,256,256]{2,1,0:T(8,128)(2,1)}), bf16[16,256,256]{2,1,0:T(8,128)(2,1)S(1)}, u32[]{:S(2)}, u32[]{:S(2)}) async-start(bf16[16,256,256]{2,1,0:T(8,128)(2,1)} %mix.1), calls=%async_computation.21 | async-start | bytes 4194304 | tf_op jit(solution)/shard_map/all_to_all | solution.py:387
  68.2 0.1 reshape.250
  68.3 0.7 compare_reduce_fusion
  69.0 0.2 select_reduce_fusion
  69.2 0.1 reshape.251
  69.4 0.1 reshape.252
  69.5 0.1 reshape.249
  69.8 0.7 slice_reduce_fusion
  70.5 2.0 fusion.9
  73.9 0.1 lt.109
  74.0 0.1 lt.111
  74.1 0.1 lt.112
  74.2 0.1 lt.114
  74.3 0.1 lt.115
  74.4 0.1 add.130
  74.5 0.1 add.131
  74.7 0.1 add.133
  74.8 0.1 add.134
  74.9 25.5 %all-to-all-done.21 = bf16[16,256,256]{2,1,0:T(8,128)(2,1)S(1)} async-done(((bf16[16,256,256]{2,1,0:T(8,128)(2,1)}), bf16[16,256,256]{2,1,0:T(8,128)(2,1)S(1)}, u32[]{:S(2)}, u32[]{:S(2)}) %all-to-all-start.21) | async-done | bytes 2097184 | tf_op jit(solution)/shard_map/all_to_all | solution.py:387
  100.4 80.2 %conditional.2 = (bf16[16,16,16,256]{3,2,1,0:T(8,128)(2,1)S(1)}) conditional(s32[]{:T(128)} %clamp.7, (bf16[16,256,256]{2,1,0:T(8,128)(2,1)S(1)}, s32[1]{0:T(128)}, s32[16,1,256]{2,1,0:T(1,128)S(1)}) %tuple.80, (bf16[16,256,256]{2,1,0:T(8,128)(2,1)S(1)}, s32[1]{0:T(128)}, s32[16,1,256]{2,1,0:T(1,128)S(1)}) %tuple.80, ...), branch_computations={%region_10.11_spmd, %region_11.12_spmd, %region_12.13_spmd, %regio... | conditional | bytes 4194312 | solution.py:413
  100.4 2.8 branch_4_fun.4
  103.2 72.5 %all_to_all.99.rows = bf16[16,176,256]{2,1,0:T(8,128)(2,1)} all-to-all(bf16[16,176,256]{2,1,0:T(8,128)(2,1)} %branch_4_fun.4), channel_id=1, replica_groups={{0,2,4,6,8,10,12,14,16,18,20,22,24,26,28,30},{1,3,5,7,9,11,13,15,17,19,..., dimensions={0} | all-to-all | bytes 2883584 | tf_op jit(solution)/shard_map/cond/branch_4_fun/all_to_all | solution.py:298
  175.7 4.9 %branch_4_fun.5 = bf16[16,16,16,256]{3,2,1,0:T(8,128)(2,1)S(1)} custom-call(bf16[16,176,256]{2,1,0:T(8,128)(2,1)} %all_to_all.99.rows, s32[16,1,256]{2,1,0:T(1,128)S(1)} %get-tuple-element.180.place), custom_call_target="tpu_custom_call" | custom-call | tf_op jit(solution)/shard_map/cond/branch_4_fun/pallas_call | solution.py:235
  180.6 85.4 %conditional.3 = (bf16[16,16,16,256]{3,2,1,0:T(8,128)(2,1)S(1)}) conditional(s32[]{:T(128)} %clamp.6, (s32[256]{0:T(256)S(1)}, bf16[16,16,16,256]{3,2,1,0:T(8,128)(2,1)S(1)}, s32[16,1,256]{2,1,0:T(1,128)S(1)}, s32[1]{0:T(128)}) %tuple.81, (s32[256]{0:T(256)S(1)}, bf16[16,16,16,256]{3,2,1,0:T(8,128)(2,1)S(1)}, ...), branch_computations={%region_20.21_spmd, %region_21.22_spmd, %region_22.23_spmd, %regio... | conditional | bytes 4194312 | solution.py:413
  180.9 4.9 %branch_5_fun.6 = bf16[16,184,256]{2,1,0:T(8,128)(2,1)} custom-call(s32[256]{0:T(256)S(1)} %get-tuple-element.219.source, bf16[16,16,16,256]{3,2,1,0:T(8,128)(2,1)S(1)} %get-tuple-element.220.rows, s32[16,1,256]{2,1,0:T(1,128)S(1)} %get-tuple-element.221.place), custom_call_target="tpu_custom_call" | custom-call | tf_op jit(solution)/shard_map/cond/branch_5_fun/pallas_call | solution.py:235
  185.7 76.9 %all_to_all.110.rows = bf16[16,184,256]{2,1,0:T(8,128)(2,1)} all-to-all(bf16[16,184,256]{2,1,0:T(8,128)(2,1)} %branch_5_fun.6), channel_id=1, replica_groups={{0,2,4,6,8,10,12,14,16,18,20,22,24,26,28,30},{1,3,5,7,9,11,13,15,17,19,..., dimensions={0} | all-to-all | bytes 3014656 | tf_op jit(solution)/shard_map/cond/branch_5_fun/all_to_all | solution.py:298
  262.6 3.4 %branch_5_fun.7 = bf16[16,16,16,256]{3,2,1,0:T(8,128)(2,1)S(1)} custom-call(s32[1]{0:T(128)} %get-tuple-element.218.sc, bf16[16,184,256]{2,1,0:T(8,128)(2,1)} %all_to_all.110.rows, s32[16,1,256]{2,1,0:T(1,128)S(1)} %get-tuple-element.221.place), custom_call_target="tpu_custom_call" | custom-call | tf_op jit(solution)/shard_map/cond/branch_5_fun/pallas_call | solution.py:235
  266.1 1.3 copy-done.1
  267.4 3.7 %all-to-all-start.22 = ((bf16[16,256,256]{2,1,0:T(8,128)(2,1)}), bf16[16,256,256]{2,1,0:T(8,128)(2,1)S(1)}, u32[]{:S(2)}, u32[]{:S(2)}) async-start(bf16[16,256,256]{2,1,0:T(8,128)(2,1)} %bitcast.40), calls=%async_computation.22 | async-start | bytes 4194304 | tf_op jit(solution)/shard_map/all_to_all | solution.py:417
  271.8 0.6 dynamic_slice.24
  273.0 0.6 pad_add_fusion.sc
  273.7 20.5 %all-to-all-done.22.rows = bf16[16,256,256]{2,1,0:T(8,128)(2,1)S(1)} async-done(((bf16[16,256,256]{2,1,0:T(8,128)(2,1)}), bf16[16,256,256]{2,1,0:T(8,128)(2,1)S(1)}, u32[]{:S(2)}, u32[]{:S(2)}) %all-to-all-start.22) | async-done | bytes 2097184 | tf_op jit(solution)/shard_map/all_to_all | solution.py:417
  294.2 1.3 copy-done
  295.5 5.0 %shard_map.156 = (bf16[128,4096]{1,0:T(8,128)(2,1)}, bf16[128,4096]{1,0:T(8,128)(2,1)}) custom-call(s32[3]{0:T(128)} %pad_add_fusion.sc, bf16[16,256,256]{2,1,0:T(8,128)(2,1)} %copy-done), custom_call_target="tpu_custom_call" | custom-call | tf_op jit(solution)/shard_map/pallas_call | solution.py:235
  300.5 10.5 %collective-permute-start.4 = (bf16[128,4096]{1,0:T(8,128)(2,1)}, bf16[128,4096]{1,0:T(8,128)(2,1)S(1)}, u32[]{:S(2)}, u32[]{:S(2)}) collective-permute-start(bf16[128,4096]{1,0:T(8,128)(2,1)} %get-tuple-element.257), channel_id=1, source_target_pairs={{0,1},{1,0},{2,3},{3,2},{4,5},{5,4},{6,7},{7,6},{8,9},{9,8},{10,11... | collective-permute-start | bytes 3145736 | tf_op jit(solution)/shard_map/ppermute | solution.py:426
  311.0 2.5 collective-permute-done.4.oth
  313.5 1.0 copy-done.2
  314.5 4.7 %norm.1 = bf16[128,8192]{1,0:T(8,128)(2,1)} custom-call(s32[3]{0:T(128)} %pad_add_fusion.sc, bf16[128,4096]{1,0:T(8,128)(2,1)} %get-tuple-element.256.own, bf16[128,4096]{1,0:T(8,128)(2,1)} %copy-done.2, f32[1,8192]{1,0:T(1,128)} %bitcast.43), custom_call_target="tpu_custom_call" | custom-call | tf_op jit(solution)/shard_map/norm/pallas_call | solution.py:428
  (40 shorter events, 0.6 us)
Async XLA Ops:
  0.0 30.1 %copy-start.4 = (bf16[128,128]{1,0:T(8,128)(2,1)S(1)}, bf16[128,128]{1,0:T(8,128)(2,1)}, u32[]{:S(2)}) copy-start(bf16[128,128]{1,0:T(8,128)(2,1)} %param.38) | copy-start | bytes 98308
  0.0 26.6 %copy-start.8 = (s32[256]{0:T(256)S(1)}, s32[256]{0:T(256)}, u32[]{:S(2)}) copy-start(s32[256]{0:T(256)} %param.47) | copy-start | bytes 3076
  0.0 28.0 %copy-start.10 = (f32[256]{0:T(256)S(1)}, f32[256]{0:T(256)}, u32[]{:S(2)}) copy-start(f32[256]{0:T(256)} %param.45) | copy-start | bytes 3076
  0.0 28.0 %copy-start.7 = (f32[4,256]{1,0:T(4,128)S(1)}, f32[4,256]{1,0:T(4,128)}, u32[]{:S(2)}) copy-start(f32[4,256]{1,0:T(4,128)} %param.44) | copy-start | bytes 12292
  0.0 30.0 %copy-start.13 = (f32[128]{0:T(128)S(1)}, f32[128]{0:T(128)}, u32[]{:S(2)}) copy-start(f32[128]{0:T(128)} %param.39) | copy-start | bytes 1540
  0.9 29.2 %collective-permute-start.2 = (bf16[128,64]{1,0:T(8,128)(2,1)S(1)}, bf16[128,64]{1,0:T(8,128)(2,1)S(1)}, u32[]{:S(2)}, u32[]{:S(2)}) collective-permute-start(bf16[128,64]{1,0:T(8,128)(2,1)S(1)} %constant_dynamic-slice_fusion.2), channel_id=1, source_target_pairs={{0,1},{1,0},{2,3},{3,2},{4,5},{5,4},{6,7},{7,6},{8,9},{9,8},{10,11... | collective-permute-start | bytes 49160 | tf_op jit(solution)/shard_map/ppermute | solution.py:284
  9.7 21.4 %collective-permute-start.1 = (bf16[128,256]{1,0:T(8,128)(2,1)}, bf16[128,256]{1,0:T(8,128)(2,1)S(1)}, u32[]{:S(2)}, u32[]{:S(2)}) collective-permute-start(bf16[128,256]{1,0:T(8,128)(2,1)} %bc_own.1), channel_id=1, source_target_pairs={{0,1},{1,0},{2,3},{3,2},{4,5},{5,4},{6,7},{7,6},{8,9},{9,8},{10,11... | collective-permute-start | bytes 196616 | tf_op jit(solution)/shard_map/ppermute | solution.py:283
  13.0 21.6 %all-to-all-start.20 = ((f32[16,8,256]{2,1,0:T(8,128)}), f32[16,8,256]{2,1,0:T(8,128)S(1)}, u32[]{:S(2)}, u32[]{:S(2)}) async-start(f32[16,8,256]{2,1,0:T(8,128)} %shard_map.154), calls=%async_computation.20 | async-start | bytes 262144 | tf_op jit(solution)/shard_map/all_to_all | solution.py:298
  23.9 17.5 %collective-permute-start = (bf16[128,4096]{1,0:T(8,128)(2,1)S(1)}, bf16[128,4096]{1,0:T(8,128)(2,1)S(1)}, u32[]{:S(2)}, u32[]{:S(2)}) collective-permute-start(bf16[128,4096]{1,0:T(8,128)(2,1)S(1)} %constant_dynamic-slice_fusion.3), channel_id=1, source_target_pairs={{0,1},{1,0},{2,3},{3,2},{4,5},{5,4},{6,7},{7,6},{8,9},{9,8},{10,11... | collective-permute-start | bytes 3145736 | tf_op jit(solution)/shard_map/ppermute | solution.py:280
  31.1 0.6 copy-start.6
  35.2 6.1 %collective-permute-start.3 = (f32[8,8,256]{2,1,0:T(8,128)S(1)}, f32[8,8,256]{2,1,0:T(8,128)S(1)}, u32[]{:S(2)}, u32[]{:S(2)}) collective-permute-start(f32[8,8,256]{2,1,0:T(8,128)S(1)} %get-tuple-element.265), channel_id=1, source_target_pairs={{0,1},{1,0},{2,3},{3,2},{4,5},{5,4},{6,7},{7,6},{8,9},{9,8},{10,11... | collective-permute-start | bytes 196616 | tf_op jit(solution)/shard_map/ppermute | solution.py:370
  41.3 0.6 copy-start.5
  41.3 1.0 copy-start.3
  61.3 6.9 %copy-start.9 = (s32[256]{0:T(256)S(1)}, s32[256]{0:T(256)}, u32[]{:S(2)}) copy-start(s32[256]{0:T(256)} %param.48) | copy-start | bytes 3076
  61.3 7.0 %copy-start.11 = (s32[256]{0:T(256)S(1)}, s32[256]{0:T(256)}, u32[]{:S(2)}) copy-start(s32[256]{0:T(256)} %param.49) | copy-start | bytes 3076
  61.3 9.2 %copy-start.12 = (s32[9]{0:T(128)S(1)}, s32[9]{0:T(128)}, u32[]{:S(2)}) copy-start(s32[9]{0:T(128)} %constant.115.clone) | copy-start | bytes 112
  61.3 39.1 %all-to-all-start.21 = ((bf16[16,256,256]{2,1,0:T(8,128)(2,1)}), bf16[16,256,256]{2,1,0:T(8,128)(2,1)S(1)}, u32[]{:S(2)}, u32[]{:S(2)}) async-start(bf16[16,256,256]{2,1,0:T(8,128)(2,1)} %mix.1), calls=%async_computation.21 | async-start | bytes 4194304 | tf_op jit(solution)/shard_map/all_to_all | solution.py:387
  266.0 1.3 copy-start.1
  267.4 26.8 %all-to-all-start.22 = ((bf16[16,256,256]{2,1,0:T(8,128)(2,1)}), bf16[16,256,256]{2,1,0:T(8,128)(2,1)S(1)}, u32[]{:S(2)}, u32[]{:S(2)}) async-start(bf16[16,256,256]{2,1,0:T(8,128)(2,1)} %bitcast.40), calls=%async_computation.22 | async-start | bytes 4194304 | tf_op jit(solution)/shard_map/all_to_all | solution.py:417
  294.2 1.3 copy-start
  300.5 13.0 %collective-permute-start.4 = (bf16[128,4096]{1,0:T(8,128)(2,1)}, bf16[128,4096]{1,0:T(8,128)(2,1)S(1)}, u32[]{:S(2)}, u32[]{:S(2)}) collective-permute-start(bf16[128,4096]{1,0:T(8,128)(2,1)} %get-tuple-element.257), channel_id=1, source_target_pairs={{0,1},{1,0},{2,3},{3,2},{4,5},{5,4},{6,7},{7,6},{8,9},{9,8},{10,11... | collective-permute-start | bytes 3145736 | tf_op jit(solution)/shard_map/ppermute | solution.py:426
  313.5 1.0 copy-start.2

commit v3 on v2

--- a/solution.py
+++ b/solution.py
@@ -20,7 +20,9 @@
         back = count - 1 - k
         moved = values
         if back:
-            moved = jnp.where(rows >= back, pltpu.roll(values, back, 0), 0.0)
+            moved = pltpu.roll(values, back, 0)
+            top = jnp.where(rows[:8] >= back, moved[:8], 0.0)
+            moved = jnp.concatenate([top, moved[8:]], axis=0)
         total = total + taps[k : k + 1] * moved
     low = 0.5 * total
     return low + low * jnp.tanh(low)
@@ -80,43 +82,50 @@
 ):
     core, used = sc[0], sc[1]
     j = pl.program_id(0)
-    half, width = x_own.shape
+    half, both_width = x_own.shape
+    columns = pl.ds(pl.multiple_of(j * both_width, both_width), both_width)
+    x_two, rows_two = joined(core, used, x_own[...], x_oth[:, columns], joint)
+    width = both_width // 2
     length = 2 * half
-    columns = pl.ds(pl.multiple_of(j * width, width), width)
-    x, rows = joined(core, used, x_own[...], x_oth[:, columns], joint)
-    w = jnp.where(j % 2 == core, w_own[j // 2], w_oth[j // 2])
-    x_act = conv_silu(x, w[0:4], w[4:5], rows)
-    at = pl.ds(pl.multiple_of(8 * j, 8), 8)
     dim = width // heads
-    rates = -jnp.exp(w[6:7])
-    sums_here = summed[at]
-    scaled = [sums_here[h : h + 1] * rates[:, h * dim : h * dim + 1] for h in range(heads)]
-    decay_rows = jnp.concatenate(scaled + [sums_here[heads:]], axis=0)
-    decay_cols = jnp.transpose(decay_rows)
-    step_cols = jnp.transpose(step[at])
     pair = 2 * dim
     first = lax.broadcasted_iota(jnp.int32, (length, pair), 1) < dim
-    mixed = []
-    for p in range(heads // 2):
-        steps = jnp.where(
-            first, step_cols[:, 2 * p : 2 * p + 1], step_cols[:, 2 * p + 1 : 2 * p + 2]
-        )
-        fed = x_act[:, p * pair : (p + 1) * pair] * steps
-        fed_hi = fed.astype(BF16)
-        fed_lo = (fed - fed_hi.astype(F32)).astype(BF16)
-        fed_both = jnp.concatenate([fed_hi, fed_lo], axis=1)
-        sums = []
-        for h in (2 * p, 2 * p + 1):
-            parts = []
-            for lo, hi in ((0, half), (half, length)):
-                gap = decay_cols[lo:hi, h : h + 1] - decay_rows[h : h + 1, :hi]
-                weight = scores[lo:hi, :hi] * jnp.exp2(jnp.minimum(gap, 0.0))
-                both = jnp.dot(weight.astype(BF16), fed_both[:hi], preferred_element_type=F32)
-                parts.append(both[:, :pair] + both[:, pair:])
-            sums.append(jnp.concatenate(parts, axis=0))
-        mixed.append(jnp.where(first, sums[0], sums[1]))
-    result = jnp.concatenate(mixed, axis=1) + w[5:6] * x_act
-    out[0] = jnp.dot(pick[...], result.astype(BF16), preferred_element_type=F32).astype(BF16)
+    for q in range(2):
+        x, rows = x_two[:, q * width : (q + 1) * width], rows_two[:, :width]
+        w = jnp.where(core == q, w_own[j], w_oth[j])
+        x_act = conv_silu(x, w[0:4], w[4:5], rows)
+        at = pl.ds(pl.multiple_of(16 * j + 8 * q, 8), 8)
+        rates = -jnp.exp(w[6:7])
+        sums_here = summed[at]
+        scaled = [sums_here[h : h + 1] * rates[:, h * dim : h * dim + 1] for h in range(heads)]
+        decay_rows = jnp.concatenate(scaled + [sums_here[heads:]], axis=0)
+        decay_cols = jnp.transpose(decay_rows)
+        step_cols = jnp.transpose(step[at])
+        mixed = []
+        for p in range(heads // 2):
+            steps = jnp.where(
+                first, step_cols[:, 2 * p : 2 * p + 1], step_cols[:, 2 * p + 1 : 2 * p + 2]
+            )
+            fed = x_act[:, p * pair : (p + 1) * pair] * steps
+            fed_hi = fed.astype(BF16)
+            fed_lo = (fed - fed_hi.astype(F32)).astype(BF16)
+            fed_both = jnp.concatenate([fed_hi, fed_lo], axis=1)
+            sums = []
+            for h in (2 * p, 2 * p + 1):
+                parts = []
+                for lo, hi in ((0, half), (half, length)):
+                    gap = decay_cols[lo:hi, h : h + 1] - decay_rows[h : h + 1, :hi]
+                    weight = scores[lo:hi, :hi] * jnp.exp2(jnp.minimum(gap, 0.0))
+                    both = jnp.dot(
+                        weight.astype(BF16), fed_both[:hi], preferred_element_type=F32
+                    )
+                    parts.append(both[:, :pair] + both[:, pair:])
+                sums.append(jnp.concatenate(parts, axis=0))
+            mixed.append(jnp.where(first, sums[0], sums[1]))
+        result = jnp.concatenate(mixed, axis=1) + w[5:6] * x_act
+        out[q] = jnp.dot(
+            pick[...], result.astype(BF16), preferred_element_type=F32
+        ).astype(BF16)
 
 
 def one_hot(size, place):
@@ -231,6 +240,10 @@
     return pl.BlockSpec(memory_space=pltpu.VMEM)
 
 
+def limits():
+    return pltpu.CompilerParams(vmem_limit_bytes=24 << 20)
+
+
 def once(kernel, scalars, outs, *operands, scratch=()):
     return pl.pallas_call(
         kernel,
@@ -239,6 +252,7 @@
         + [resident()] * (len(operands) - scalars),
         out_specs=jax.tree.map(lambda _: resident(), outs),
         scratch_shapes=list(scratch),
+        compiler_params=limits(),
     )(*operands)
 
 
@@ -375,12 +389,13 @@
         out_shape=jax.ShapeDtypeStruct((chunks, length, width), BF16),
         grid_spec=grid_spec(
             1,
-            (chunks,),
-            [pl.BlockSpec((half, width), lambda j, sc: (0, sc[0] * chunks + j))]
+            (chunks // 2,),
+            [pl.BlockSpec((half, 2 * width), lambda j, sc: (0, sc[0] * (chunks // 2) + j))]
             + [resident()] * 7,
-            pl.BlockSpec((1, length, width), lambda j, sc: (j, 0, 0)),
-            [pltpu.VMEM((2, half, width), BF16)],
+            pl.BlockSpec((2, length, width), lambda j, sc: (j, 0, 0)),
+            [pltpu.VMEM((2, half, 2 * width), BF16)],
         ),
+        compiler_params=limits(),
         name="mix",
     )(where_am_i, x_in, x_oth, w_own, w_oth, step_t, scores, summed, pick)
 
@@ -434,6 +449,7 @@
             [resident()] * 3,
             pl.BlockSpec((step_rows, channels), lambda i, sc: (i, 0)),
         ),
+        compiler_params=limits(),
         name="norm",
     )(ends_at, own, got, norm_gain[None])
 

time: 324 us -> 305 us (0.941); the launches traced: 319 us -> 306 us
  Pallas kernels: 48.5 us -> 34.5 us
  local copies, waits for them, and re-layouts: 11.2 us -> 15.4 us
    pallas_call x7, Pallas kernels: 24.8 us -> 17.4 us  [once(): pl.pallas_call(kernel, out_shape=outs, in_specs=[pl.BlockSpec(memory_spac...]
    pallas_call x1, Pallas kernels: 19 us -> 14.1 us  [per_device(): pl.pallas_call(functools.partial(mix_kernel, heads), out_shape=jax.ShapeD...]
    unnamed x28 -> x42, local copies, waits for them, and re-layouts: 5.3 us -> 8.09 us
  transfers between devices with their start and end apart: 8 -> 8, of which waited for: 5 -> 4; matrix products, arithmetic and copies ran while one was open for 4% -> 4% of each run, Pallas kernels for 1% -> 1%
where the time goes in v3:
time: 305 us; the launch traced here: 306 us
  blocking collectives  149 us (49%)
  waiting for transfers between devices  49.9 us (16%)
  starting transfers between devices  48.7 us (16%)
  Pallas kernels  34.5 us (11%)
  local copies, waits for them, and re-layouts  15.4 us (5%)
  other arithmetic  5.54 us (2%)
    all_to_all x2, blocking collectives, exchange(): lax.all_to_all(a, 'ch', split_axis=0, concat_axis=0, axis_index_groups=ri...  149 us
    all_to_all x1, waiting for transfers between devices, per_device(): lax.all_to_all(mixed, 'grp', split_axis=0, concat_axis=0, tiled=True)  25.5 us
    all_to_all x1, waiting for transfers between devices, per_device(): lax.all_to_all(landed, 'grp', split_axis=0, concat_axis=0, tiled=True)  21.2 us
    pallas_call x7, Pallas kernels, once(): pl.pallas_call(kernel, out_shape=outs, in_specs=[pl.BlockSpec(memory_spac...  17.4 us
    pallas_call x1, Pallas kernels, per_device(): pl.pallas_call(functools.partial(mix_kernel, heads), out_shape=jax.ShapeD...  14.1 us
    ppermute x1, starting transfers between devices, per_device(): got = lax.ppermute(oth, 'ch', swap)  10.4 us
    all_to_all x1, starting transfers between devices, exchange(): lax.all_to_all(a, 'ch', split_axis=0, concat_axis=0, axis_index_groups=ri...  9.62 us
    ppermute x1, starting transfers between devices, per_device(): lax.ppermute(lax.dynamic_slice_in_dim(dt_in, other_half * head_half, head...  8.74 us
  transfers between devices with their start and end apart: 8, of which 4 were waited for; matrix products, arithmetic and copies ran while one was open for 4% of the time, Pallas kernels for 1%

profile of v3, /device:TPU:1, one launch (start us, length us, event | category | flops | bytes accessed | tf_op | source)
XLA Modules:
  0.0 306.2 jit_solution(3580990815508632291)
XLA Ops:
  0.0 1.0 constant_dynamic-slice_fusion.2
  1.0 8.7 %collective-permute-start.2 = (bf16[128,64]{1,0:T(8,128)(2,1)S(1)}, bf16[128,64]{1,0:T(8,128)(2,1)S(1)}, u32[]{:S(2)}, u32[]{:S(2)}) collective-permute-start(bf16[128,64]{1,0:T(8,128)(2,1)S(1)} %constant_dynamic-slice_fusion.2), channel_id=1, source_target_pairs={{0,1},{1,0},{2,3},{3,2},{4,5},{5,4},{6,7},{7,6},{8,9},{9,8},{10,11... | collective-permute-start | bytes 49160 | tf_op jit(solution)/shard_map/ppermute | solution.py:298
  9.7 1.9 collective-permute-start.1
  11.7 0.7 copy-done.9
  12.4 0.7 copy-done.10
  13.0 0.7 copy-done.11
  13.7 0.7 copy-done.12
  14.4 1.2 shard_map.154
  15.6 9.6 %all-to-all-start.20 = ((f32[16,8,256]{2,1,0:T(8,128)}), f32[16,8,256]{2,1,0:T(8,128)}, u32[]{:S(2)}, u32[]{:S(2)}) async-start(f32[16,8,256]{2,1,0:T(8,128)} %shard_map.154), calls=%async_computation.20 | async-start | bytes 262144 | tf_op jit(solution)/shard_map/all_to_all | solution.py:312
  25.2 2.3 constant_dynamic-slice_fusion.3
  27.5 2.7 collective-permute-start
  30.2 0.7 dynamic_slice.25
  30.9 0.7 compare_convert_fusion
  31.8 0.8 pad_add_fusion.1.sc
  32.6 0.1 broadcast_select_fusion.1
  32.7 0.1 fusion.2
  32.8 0.1 copy.38
  33.0 0.6 copy-done.6
  33.6 0.8 copy-done.5
  34.4 0.8 copy-done.7
  35.3 1.2 shard_map.155
  36.5 0.6 copy-done.1
  37.1 0.6 copy-done.3
  37.8 0.9 constant_dynamic-slice_fusion
  38.7 4.7 %collective-permute-start.3 = (f32[8,8,256]{2,1,0:T(8,128)S(1)}, f32[8,8,256]{2,1,0:T(8,128)S(1)}, u32[]{:S(2)}, u32[]{:S(2)}) collective-permute-start(f32[8,8,256]{2,1,0:T(8,128)S(1)} %get-tuple-element.265), channel_id=1, source_target_pairs={{0,1},{1,0},{2,3},{3,2},{4,5},{5,4},{6,7},{7,6},{8,9},{9,8},{10,11... | collective-permute-start | bytes 196616 | tf_op jit(solution)/shard_map/ppermute | solution.py:384
  43.4 0.9 collective-permute-done.3.w_oth
  44.3 0.9 copy-done.2
  45.2 0.9 copy-done.4
  46.1 14.1 %mix.1 = bf16[16,256,256]{2,1,0:T(8,128)(2,1)} custom-call(s32[2]{0:T(128)S(1)} %pad_add_fusion.1.sc, bf16[128,8192]{1,0:T(8,128)(2,1)S(1)} %copy-done, bf16[128,4096]{1,0:T(8,128)(2,1)S(1)} %collective-permute-done.x_oth, f32[8,8,256]{2,1,0:T(8,128)S(1)} %get-tuple-element.266.w_own, f32[8,8,256]{2,1,0:T(8,128)S(1)} %collective-permute-done.3.w_oth, ...), custom_call_target="tpu_custom_call" | custom-call | tf_op jit(solution)/shard_map/mix/pallas_call | solution.py:387
  60.3 6.9 %all-to-all-start.21 = ((bf16[16,256,256]{2,1,0:T(8,128)(2,1)}), bf16[16,256,256]{2,1,0:T(8,128)(2,1)S(1)}, u32[]{:S(2)}, u32[]{:S(2)}) async-start(bf16[16,256,256]{2,1,0:T(8,128)(2,1)} %mix.1), calls=%async_computation.21 | async-start | bytes 4194304 | tf_op jit(solution)/shard_map/all_to_all | solution.py:402
  67.2 0.1 reshape.250
  67.3 0.7 compare_reduce_fusion
  68.0 0.2 select_reduce_fusion
  68.2 0.1 reshape.251
  68.3 0.1 reshape.252
  68.4 0.1 reshape.249
  68.7 0.7 slice_reduce_fusion
  69.5 1.9 fusion.9
  72.9 0.1 lt.109
  73.0 0.1 lt.111
  73.1 0.1 lt.112
  73.2 0.1 lt.114
  73.3 0.1 lt.115
  73.4 0.1 add.130
  73.5 0.1 add.131
  73.6 0.1 add.133
  73.7 0.1 add.134
  73.9 25.5 %all-to-all-done.21 = bf16[16,256,256]{2,1,0:T(8,128)(2,1)S(1)} async-done(((bf16[16,256,256]{2,1,0:T(8,128)(2,1)}), bf16[16,256,256]{2,1,0:T(8,128)(2,1)S(1)}, u32[]{:S(2)}, u32[]{:S(2)}) %all-to-all-start.21) | async-done | bytes 2097184 | tf_op jit(solution)/shard_map/all_to_all | solution.py:402
  99.4 75.3 %conditional.2 = (bf16[16,16,16,256]{3,2,1,0:T(8,128)(2,1)S(1)}) conditional(s32[]{:T(128)} %clamp.7, (bf16[16,256,256]{2,1,0:T(8,128)(2,1)S(1)}, s32[1]{0:T(128)}, s32[16,1,256]{2,1,0:T(1,128)S(1)}) %tuple.80, (bf16[16,256,256]{2,1,0:T(8,128)(2,1)S(1)}, s32[1]{0:T(128)}, s32[16,1,256]{2,1,0:T(1,128)S(1)}) %tuple.80, ...), branch_computations={%region_10.11_spmd, %region_11.12_spmd, %region_12.13_spmd, %regio... | conditional | bytes 4194312 | solution.py:428
  99.4 1.7 branch_3_fun.4
  101.1 70.1 %all_to_all.98.rows = bf16[16,168,256]{2,1,0:T(8,128)(2,1)S(1)} all-to-all(bf16[16,168,256]{2,1,0:T(8,128)(2,1)S(1)} %branch_3_fun.4), channel_id=1, replica_groups={{0,2,4,6,8,10,12,14,16,18,20,22,24,26,28,30},{1,3,5,7,9,11,13,15,17,19,..., dimensions={0} | all-to-all | bytes 2752512 | tf_op jit(solution)/shard_map/cond/branch_3_fun/all_to_all | solution.py:312
  171.1 3.5 %branch_3_fun.5 = bf16[16,16,16,256]{3,2,1,0:T(8,128)(2,1)S(1)} custom-call(bf16[16,168,256]{2,1,0:T(8,128)(2,1)S(1)} %all_to_all.98.rows, s32[16,1,256]{2,1,0:T(1,128)S(1)} %get-tuple-element.172.place), custom_call_target="tpu_custom_call" | custom-call | tf_op jit(solution)/shard_map/cond/branch_3_fun/pallas_call | solution.py:248
  174.7 86.2 %conditional.3 = (bf16[16,16,16,256]{3,2,1,0:T(8,128)(2,1)}) conditional(s32[]{:T(128)} %clamp.6, (s32[256]{0:T(256)S(1)}, bf16[16,16,16,256]{3,2,1,0:T(8,128)(2,1)S(1)}, s32[16,1,256]{2,1,0:T(1,128)S(1)}, s32[1]{0:T(128)}) %tuple.81, (s32[256]{0:T(256)S(1)}, bf16[16,16,16,256]{3,2,1,0:T(8,128)(2,1)S(1)}, ...), branch_computations={%region_20.21_spmd, %region_21.22_spmd, %region_22.23_spmd, %regio... | conditional | bytes 4194312 | solution.py:428
  174.9 3.7 %branch_6_fun.6 = bf16[16,192,256]{2,1,0:T(8,128)(2,1)S(1)} custom-call(s32[256]{0:T(256)S(1)} %get-tuple-element.223.source, bf16[16,16,16,256]{3,2,1,0:T(8,128)(2,1)S(1)} %get-tuple-element.224.rows, s32[16,1,256]{2,1,0:T(1,128)S(1)} %get-tuple-element.225.place), custom_call_target="tpu_custom_call" | custom-call | tf_op jit(solution)/shard_map/cond/branch_6_fun/pallas_call | solution.py:248
  178.7 78.9 %all_to_all.111.rows = bf16[16,192,256]{2,1,0:T(8,128)(2,1)S(1)} all-to-all(bf16[16,192,256]{2,1,0:T(8,128)(2,1)S(1)} %branch_6_fun.6), channel_id=1, replica_groups={{0,2,4,6,8,10,12,14,16,18,20,22,24,26,28,30},{1,3,5,7,9,11,13,15,17,19,..., dimensions={0} | all-to-all | bytes 3145728 | tf_op jit(solution)/shard_map/cond/branch_6_fun/all_to_all | solution.py:312
  257.5 3.3 %branch_6_fun.7 = bf16[16,16,16,256]{3,2,1,0:T(8,128)(2,1)} custom-call(s32[1]{0:T(128)} %get-tuple-element.222.sc, bf16[16,192,256]{2,1,0:T(8,128)(2,1)S(1)} %all_to_all.111.rows, s32[16,1,256]{2,1,0:T(1,128)S(1)} %get-tuple-element.225.place), custom_call_target="tpu_custom_call" | custom-call | tf_op jit(solution)/shard_map/cond/branch_6_fun/pallas_call | solution.py:248
  260.9 3.7 %all-to-all-start.22 = ((bf16[16,256,256]{2,1,0:T(8,128)(2,1)}), bf16[16,256,256]{2,1,0:T(8,128)(2,1)S(1)}, u32[]{:S(2)}, u32[]{:S(2)}) async-start(bf16[16,256,256]{2,1,0:T(8,128)(2,1)} %bitcast.23), calls=%async_computation.22 | async-start | bytes 4194304 | tf_op jit(solution)/shard_map/all_to_all | solution.py:432
  265.3 0.7 dynamic_slice.24
  266.5 0.1 pad_add_fusion.sc
  266.6 21.2 %all-to-all-done.22.rows = bf16[16,256,256]{2,1,0:T(8,128)(2,1)S(1)} async-done(((bf16[16,256,256]{2,1,0:T(8,128)(2,1)}), bf16[16,256,256]{2,1,0:T(8,128)(2,1)S(1)}, u32[]{:S(2)}, u32[]{:S(2)}) %all-to-all-start.22) | async-done | bytes 2097184 | tf_op jit(solution)/shard_map/all_to_all | solution.py:432
  287.8 2.6 shard_map.156
  290.4 10.4 %collective-permute-start.4 = (bf16[128,4096]{1,0:T(8,128)(2,1)S(1)}, bf16[128,4096]{1,0:T(8,128)(2,1)S(1)}, u32[]{:S(2)}, u32[]{:S(2)}) collective-permute-start(bf16[128,4096]{1,0:T(8,128)(2,1)S(1)} %get-tuple-element.257), channel_id=1, source_target_pairs={{0,1},{1,0},{2,3},{3,2},{4,5},{5,4},{6,7},{7,6},{8,9},{9,8},{10,11... | collective-permute-start | bytes 3145736 | tf_op jit(solution)/shard_map/ppermute | solution.py:441
  300.9 2.3 collective-permute-done.4.oth
  303.2 3.1 norm.1
  (54 shorter events, 0.8 us)
Async XLA Ops:
  0.0 44.3 %copy-start = (bf16[128,8192]{1,0:T(8,128)(2,1)S(1)}, bf16[128,8192]{1,0:T(8,128)(2,1)}, u32[]{:S(2)}) copy-start(bf16[128,8192]{1,0:T(8,128)(2,1)} %x_own.1) | copy-start | bytes 6291460
  1.0 31.6 %collective-permute-start.2 = (bf16[128,64]{1,0:T(8,128)(2,1)S(1)}, bf16[128,64]{1,0:T(8,128)(2,1)S(1)}, u32[]{:S(2)}, u32[]{:S(2)}) collective-permute-start(bf16[128,64]{1,0:T(8,128)(2,1)S(1)} %constant_dynamic-slice_fusion.2), channel_id=1, source_target_pairs={{0,1},{1,0},{2,3},{3,2},{4,5},{5,4},{6,7},{7,6},{8,9},{9,8},{10,11... | collective-permute-start | bytes 49160 | tf_op jit(solution)/shard_map/ppermute | solution.py:298
  9.7 23.2 %collective-permute-start.1 = (bf16[128,256]{1,0:T(8,128)(2,1)}, bf16[128,256]{1,0:T(8,128)(2,1)S(1)}, u32[]{:S(2)}, u32[]{:S(2)}) collective-permute-start(bf16[128,256]{1,0:T(8,128)(2,1)} %bc_own.1), channel_id=1, source_target_pairs={{0,1},{1,0},{2,3},{3,2},{4,5},{5,4},{6,7},{7,6},{8,9},{9,8},{10,11... | collective-permute-start | bytes 196616 | tf_op jit(solution)/shard_map/ppermute | solution.py:297
  11.7 0.7 copy-start.9
  12.4 0.7 copy-start.10
  13.0 0.7 copy-start.11
  13.7 0.7 copy-start.12
  14.3 15.9 %copy-start.15 = (s32[256]{0:T(256)S(1)}, s32[256]{0:T(256)}, u32[]{:S(2)}) copy-start(s32[256]{0:T(256)} %param.47) | copy-start | bytes 3076
  14.3 17.3 %copy-start.14 = (f32[4,256]{1,0:T(4,128)S(1)}, f32[4,256]{1,0:T(4,128)}, u32[]{:S(2)}) copy-start(f32[4,256]{1,0:T(4,128)} %param.44) | copy-start | bytes 12292
  14.3 17.3 %copy-start.17 = (f32[256]{0:T(256)S(1)}, f32[256]{0:T(256)}, u32[]{:S(2)}) copy-start(f32[256]{0:T(256)} %param.45) | copy-start | bytes 3076
  14.4 18.2 %copy-start.20 = (f32[128]{0:T(128)S(1)}, f32[128]{0:T(128)}, u32[]{:S(2)}) copy-start(f32[128]{0:T(128)} %param.39) | copy-start | bytes 1540
  14.4 18.2 %copy-start.13 = (bf16[128,128]{1,0:T(8,128)(2,1)S(1)}, bf16[128,128]{1,0:T(8,128)(2,1)}, u32[]{:S(2)}) copy-start(bf16[128,128]{1,0:T(8,128)(2,1)} %param.38) | copy-start | bytes 98308
  15.6 22.2 %all-to-all-start.20 = ((f32[16,8,256]{2,1,0:T(8,128)}), f32[16,8,256]{2,1,0:T(8,128)}, u32[]{:S(2)}, u32[]{:S(2)}) async-start(f32[16,8,256]{2,1,0:T(8,128)} %shard_map.154), calls=%async_computation.20 | async-start | bytes 262144 | tf_op jit(solution)/shard_map/all_to_all | solution.py:312
  27.5 16.8 %collective-permute-start = (bf16[128,4096]{1,0:T(8,128)(2,1)}, bf16[128,4096]{1,0:T(8,128)(2,1)S(1)}, u32[]{:S(2)}, u32[]{:S(2)}) collective-permute-start(bf16[128,4096]{1,0:T(8,128)(2,1)} %constant_dynamic-slice_fusion.3), channel_id=1, source_target_pairs={{0,1},{1,0},{2,3},{3,2},{4,5},{5,4},{6,7},{7,6},{8,9},{9,8},{10,11... | collective-permute-start | bytes 3145736 | tf_op jit(solution)/shard_map/ppermute | solution.py:294
  33.0 0.6 copy-start.6
  33.6 0.8 copy-start.5
  34.4 0.8 copy-start.7
  36.5 0.7 copy-start.1
  37.1 0.6 copy-start.3
  38.7 5.6 %collective-permute-start.3 = (f32[8,8,256]{2,1,0:T(8,128)S(1)}, f32[8,8,256]{2,1,0:T(8,128)S(1)}, u32[]{:S(2)}, u32[]{:S(2)}) collective-permute-start(f32[8,8,256]{2,1,0:T(8,128)S(1)} %get-tuple-element.265), channel_id=1, source_target_pairs={{0,1},{1,0},{2,3},{3,2},{4,5},{5,4},{6,7},{7,6},{8,9},{9,8},{10,11... | collective-permute-start | bytes 196616 | tf_op jit(solution)/shard_map/ppermute | solution.py:384
  44.3 0.9 copy-start.2
  45.2 0.9 copy-start.4
  60.2 6.9 %copy-start.16 = (s32[256]{0:T(256)S(1)}, s32[256]{0:T(256)}, u32[]{:S(2)}) copy-start(s32[256]{0:T(256)} %param.48) | copy-start | bytes 3076
  60.3 7.0 %copy-start.18 = (s32[256]{0:T(256)S(1)}, s32[256]{0:T(256)}, u32[]{:S(2)}) copy-start(s32[256]{0:T(256)} %param.49) | copy-start | bytes 3076
  60.3 9.2 %copy-start.19 = (s32[9]{0:T(128)S(1)}, s32[9]{0:T(128)}, u32[]{:S(2)}) copy-start(s32[9]{0:T(128)} %constant.115.clone) | copy-start | bytes 112
  60.3 39.1 %all-to-all-start.21 = ((bf16[16,256,256]{2,1,0:T(8,128)(2,1)}), bf16[16,256,256]{2,1,0:T(8,128)(2,1)S(1)}, u32[]{:S(2)}, u32[]{:S(2)}) async-start(bf16[16,256,256]{2,1,0:T(8,128)(2,1)} %mix.1), calls=%async_computation.21 | async-start | bytes 4194304 | tf_op jit(solution)/shard_map/all_to_all | solution.py:402
  260.9 27.0 %all-to-all-start.22 = ((bf16[16,256,256]{2,1,0:T(8,128)(2,1)}), bf16[16,256,256]{2,1,0:T(8,128)(2,1)S(1)}, u32[]{:S(2)}, u32[]{:S(2)}) async-start(bf16[16,256,256]{2,1,0:T(8,128)(2,1)} %bitcast.23), calls=%async_computation.22 | async-start | bytes 4194304 | tf_op jit(solution)/shard_map/all_to_all | solution.py:432
  264.6 38.5 %copy-start.8 = (f32[8192]{0:T(1024)S(1)}, f32[8192]{0:T(1024)}, u32[]{:S(2)}) copy-start(f32[8192]{0:T(1024)} %param.46) | copy-start | bytes 98308
  290.4 12.7 %collective-permute-start.4 = (bf16[128,4096]{1,0:T(8,128)(2,1)S(1)}, bf16[128,4096]{1,0:T(8,128)(2,1)S(1)}, u32[]{:S(2)}, u32[]{:S(2)}) collective-permute-start(bf16[128,4096]{1,0:T(8,128)(2,1)S(1)} %get-tuple-element.257), channel_id=1, source_target_pairs={{0,1},{1,0},{2,3},{3,2},{4,5},{5,4},{6,7},{7,6},{8,9},{9,8},{10,11... | collective-permute-start | bytes 3145736 | tf_op jit(solution)/shard_map/ppermute | solution.py:441

commit v4 on v3

--- a/solution.py
+++ b/solution.py
@@ -29,7 +29,7 @@
 
 
 def small_kernel(skip, rate, taps, bias, out):
-    count, width = out.shape[0], out.shape[2]
+    width = out.shape[1]
     heads = skip.shape[0]
     lane = lax.broadcasted_iota(jnp.int32, (1, width), 1)
 
@@ -40,9 +40,7 @@
         return spread
 
     rows = [taps[...], bias[...], by_channel(skip), by_channel(rate), jnp.zeros((1, width), F32)]
-    share = jnp.concatenate(rows, axis=0)
-    for i in range(count):
-        out[i] = share
+    out[...] = jnp.concatenate(rows, axis=0)
 
 
 def joined(core, used, own, oth, buffer):
@@ -78,7 +76,7 @@
 
 
 def mix_kernel(
-    heads, sc, x_own, x_oth, w_own, w_oth, step, scores, summed, pick, out, joint
+    heads, sc, x_own, x_oth, w_half, step, scores, summed, pick, out, joint
 ):
     core, used = sc[0], sc[1]
     j = pl.program_id(0)
@@ -92,7 +90,7 @@
     first = lax.broadcasted_iota(jnp.int32, (length, pair), 1) < dim
     for q in range(2):
         x, rows = x_two[:, q * width : (q + 1) * width], rows_two[:, :width]
-        w = jnp.where(core == q, w_own[j], w_oth[j])
+        w = w_half[2 * j + q]
         x_act = conv_silu(x, w[0:4], w[4:5], rows)
         at = pl.ds(pl.multiple_of(16 * j + 8 * q, 8), 8)
         rates = -jnp.exp(w[6:7])
@@ -244,7 +242,7 @@
     return pltpu.CompilerParams(vmem_limit_bytes=24 << 20)
 
 
-def once(kernel, scalars, outs, *operands, scratch=()):
+def once(kernel, scalars, outs, *operands, scratch=(), params=None):
     return pl.pallas_call(
         kernel,
         out_shape=outs,
@@ -252,7 +250,7 @@
         + [resident()] * (len(operands) - scalars),
         out_specs=jax.tree.map(lambda _: resident(), outs),
         scratch_shapes=list(scratch),
-        compiler_params=limits(),
+        compiler_params=params or limits(),
     )(*operands)
 
 
@@ -298,22 +296,25 @@
     dt_oth = lax.ppermute(
         lax.dynamic_slice_in_dim(dt_in, other_half * head_half, head_half, 1), "ch", swap
     )
-    shares = once(
+    share = once(
         small_kernel,
         2,
-        jax.ShapeDtypeStruct((n_z, 8, width), F32),
+        jax.ShapeDtypeStruct((8, width), F32),
         skip_d,
         a_log,
         conv_x,
         conv_x_bias[None],
-    )
+        params=pltpu.CompilerParams(),
+    )
+    to_half = [(i, 2 * (i % n_z) + i // n_z) for i in range(n_ch)]
+    share = lax.ppermute(share, "ch", to_half)
 
     def exchange(a):
         return lax.all_to_all(
             a, "ch", split_axis=0, concat_axis=0, axis_index_groups=rings, tiled=True
         )
 
-    by_chip = exchange(shares)
+    w_half = exchange(jnp.broadcast_to(share[None], (n_z, 8, width)))
     pairs = n_grp * n_z
     ids = jnp.arange(pairs, dtype=jnp.int32)
     alive = dest_group >= 0
@@ -377,13 +378,9 @@
         wbc,
         step_t,
         scratch=[pltpu.VMEM((2,) + bc_in.shape, BF16)],
-    )
-    by_chip, scores = lax.optimization_barrier((by_chip, scores))
-    n_half = n_z // 2
-    w_own = lax.dynamic_slice_in_dim(by_chip, core * n_half, n_half, 0)
-    w_oth = lax.ppermute(
-        lax.dynamic_slice_in_dim(by_chip, other_half * n_half, n_half, 0), "ch", swap
-    )
+        params=pltpu.CompilerParams(),
+    )
+    w_half, scores = lax.optimization_barrier((w_half, scores))
     mixed = pl.pallas_call(
         functools.partial(mix_kernel, heads),
         out_shape=jax.ShapeDtypeStruct((chunks, length, width), BF16),
@@ -391,13 +388,12 @@
             1,
             (chunks // 2,),
             [pl.BlockSpec((half, 2 * width), lambda j, sc: (0, sc[0] * (chunks // 2) + j))]
-            + [resident()] * 7,
+            + [resident()] * 6,
             pl.BlockSpec((2, length, width), lambda j, sc: (j, 0, 0)),
             [pltpu.VMEM((2, half, 2 * width), BF16)],
         ),
-        compiler_params=limits(),
         name="mix",
-    )(where_am_i, x_in, x_oth, w_own, w_oth, step_t, scores, summed, pick)
+    )(where_am_i, x_in, x_oth, w_half, step_t, scores, summed, pick)
 
     spread = lax.all_to_all(mixed, "grp", split_axis=0, concat_axis=0, tiled=True)
 

time: 305 us -> 308 us (level); the launches traced: 306 us -> 305 us
  local copies, waits for them, and re-layouts: 15.4 us -> 8.02 us
    all_to_all x1, waiting for transfers between devices: 0.01 us -> 7.88 us  [exchange(): lax.all_to_all(a, 'ch', split_axis=0, concat_axis=0, axis_index_groups=ri...]
    all_to_all x1, waiting for transfers between devices: 25.5 us -> 18.2 us  [per_device(): lax.all_to_all(mixed, 'grp', split_axis=0, concat_axis=0, tiled=True)]
    ppermute x1, starting transfers between devices: 8.74 us -> 1.91 us  [per_device(): lax.ppermute(lax.dynamic_slice_in_dim(dt_in, other_half * head_half, head...]
    unnamed x42 -> x28, local copies, waits for them, and re-layouts: 8.09 us -> 2.98 us
    all_to_all x1, starting transfers between devices: 9.62 us -> 13.5 us  [exchange(): lax.all_to_all(a, 'ch', split_axis=0, concat_axis=0, axis_index_groups=ri...]
where the time goes in v4:
time: 308 us; the launch traced here: 305 us
  blocking collectives  151 us (49%)
  starting transfers between devices  51.1 us (17%)
  waiting for transfers between devices  49.2 us (16%)
  Pallas kernels  36.2 us (12%)
  local copies, waits for them, and re-layouts  8.02 us (3%)
  other arithmetic  6.98 us (2%)
    all_to_all x2, blocking collectives, exchange(): lax.all_to_all(a, 'ch', split_axis=0, concat_axis=0, axis_index_groups=ri...  151 us
    all_to_all x1, waiting for transfers between devices, per_device(): lax.all_to_all(landed, 'grp', split_axis=0, concat_axis=0, tiled=True)  20.9 us
    all_to_all x1, waiting for transfers between devices, per_device(): lax.all_to_all(mixed, 'grp', split_axis=0, concat_axis=0, tiled=True)  18.2 us
    pallas_call x7, Pallas kernels, once(): pl.pallas_call(kernel, out_shape=outs, in_specs=[pl.BlockSpec(memory_spac...  17.5 us
    pallas_call x1, Pallas kernels, per_device(): pl.pallas_call(functools.partial(mix_kernel, heads), out_shape=jax.ShapeD...  15.7 us
    all_to_all x1, starting transfers between devices, exchange(): lax.all_to_all(a, 'ch', split_axis=0, concat_axis=0, axis_index_groups=ri...  13.5 us
    ppermute x1, starting transfers between devices, per_device(): got = lax.ppermute(oth, 'ch', swap)  11 us
    all_to_all x1, waiting for transfers between devices, exchange(): lax.all_to_all(a, 'ch', split_axis=0, concat_axis=0, axis_index_groups=ri...  7.88 us
  transfers between devices with their start and end apart: 8, of which 4 were waited for; matrix products, arithmetic and copies ran while one was open for 4% of the time, Pallas kernels for 1%

profile of v4, /device:TPU:1, one launch (start us, length us, event | category | flops | bytes accessed | tf_op | source)
XLA Modules:
  0.0 305.3 jit_solution(10089572988012919231)
XLA Ops:
  0.0 1.4 shard_map.154
  1.5 4.9 %collective-permute-start.1 = (f32[8,256]{1,0:T(8,128)}, f32[8,256]{1,0:T(8,128)S(1)}, u32[]{:S(2)}, u32[]{:S(2)}) collective-permute-start(f32[8,256]{1,0:T(8,128)} %shard_map.154), channel_id=1, source_target_pairs={{0,0},{1,2},{2,4},{3,6},{4,8},{5,10},{6,12},{7,14},{8,16},{9,18},{... | collective-permute-start | bytes 24584 | tf_op jit(solution)/shard_map/ppermute | solution.py:310
  6.4 1.3 constant_dynamic-slice_fusion.1
  7.7 5.1 %collective-permute-start = (bf16[128,4096]{1,0:T(8,128)(2,1)S(1)}, bf16[128,4096]{1,0:T(8,128)(2,1)S(1)}, u32[]{:S(2)}, u32[]{:S(2)}) collective-permute-start(bf16[128,4096]{1,0:T(8,128)(2,1)S(1)} %constant_dynamic-slice_fusion.1), channel_id=1, source_target_pairs={{0,1},{1,0},{2,3},{3,2},{4,5},{5,4},{6,7},{7,6},{8,9},{9,8},{10,11... | collective-permute-start | bytes 3145736 | tf_op jit(solution)/shard_map/ppermute | solution.py:292
  12.9 0.1 constant_dynamic-slice_fusion
  12.9 1.9 collective-permute-start.3
  14.9 2.4 collective-permute-start.2
  17.3 0.6 dynamic_slice.19
  17.9 0.1 pad.10.clone
  18.0 0.6 compare_convert_fusion
  18.6 0.7 maximum_maximum_fusion.wbc
  19.2 1.2 pad_add_fusion.1.sc
  20.4 0.1 dynamic_slice.23
  20.5 0.7 broadcast_in_dim.77
  21.1 13.5 %all-to-all-start.20 = ((f32[16,8,256]{2,1,0:T(8,128)}), f32[16,8,256]{2,1,0:T(8,128)S(1)}, u32[]{:S(2)}, u32[]{:S(2)}) async-start(f32[16,8,256]{2,1,0:T(8,128)} %broadcast_in_dim.77), calls=%async_computation.20 | async-start | bytes 262144 | tf_op jit(solution)/shard_map/all_to_all | solution.py:313
  34.7 0.1 broadcast_select_fusion.1
  34.8 0.1 fusion.2
  34.9 0.1 copy.38
  35.0 0.7 bitcast_convert_fusion.step
  35.7 0.6 copy-done.6
  36.3 2.5 shard_map.155
  38.8 7.9 %all-to-all-done.20.w_half = f32[16,8,256]{2,1,0:T(8,128)S(1)} async-done(((f32[16,8,256]{2,1,0:T(8,128)}), f32[16,8,256]{2,1,0:T(8,128)S(1)}, u32[]{:S(2)}, u32[]{:S(2)}) %all-to-all-start.20) | async-done | bytes 131104 | tf_op jit(solution)/shard_map/all_to_all | solution.py:313
  46.7 0.6 copy-done.3
  47.3 0.4 copy-done.2
  47.7 15.7 %mix.1 = bf16[16,256,256]{2,1,0:T(8,128)(2,1)} custom-call(s32[2]{0:T(128)} %pad_add_fusion.1.sc, bf16[128,8192]{1,0:T(8,128)(2,1)} %x_own.1, bf16[128,4096]{1,0:T(8,128)(2,1)} %copy-done.2, f32[16,8,256]{2,1,0:T(8,128)} %copy-done.3, f32[128,256]{1,0:T(8,128)} %bitcast_convert_fusion.step, f32[256,256]{1,0:T(8,128)} %get-tuple-element.251.scores, ...), custom_call_target="tpu_custom_call" | custom-call | tf_op jit(solution)/shard_map/mix/pallas_call | solution.py:384
  63.4 6.9 %all-to-all-start.21 = ((bf16[16,256,256]{2,1,0:T(8,128)(2,1)}), bf16[16,256,256]{2,1,0:T(8,128)(2,1)S(1)}, u32[]{:S(2)}, u32[]{:S(2)}) async-start(bf16[16,256,256]{2,1,0:T(8,128)(2,1)} %mix.1), calls=%async_computation.21 | async-start | bytes 4194304 | tf_op jit(solution)/shard_map/all_to_all | solution.py:398
  70.3 0.1 reshape.251
  70.4 0.6 compare_reduce_fusion
  71.0 0.2 select_reduce_fusion
  71.2 0.1 reshape.252
  71.3 0.1 copy.37
  71.4 0.1 reshape.253
  71.5 0.1 reshape.250
  71.7 0.1 copy.36
  71.7 0.1 copy.34
  71.8 0.7 slice_reduce_fusion
  72.5 1.9 fusion.9
  75.9 0.1 lt.103
  76.0 0.1 lt.105
  76.1 0.1 lt.106
  76.2 0.1 lt.108
  76.3 0.1 lt.109
  76.4 0.1 add.124
  76.5 0.1 add.125
  76.7 0.1 add.127
  76.8 0.1 add.128
  76.9 18.2 %all-to-all-done.21 = bf16[16,256,256]{2,1,0:T(8,128)(2,1)S(1)} async-done(((bf16[16,256,256]{2,1,0:T(8,128)(2,1)}), bf16[16,256,256]{2,1,0:T(8,128)(2,1)S(1)}, u32[]{:S(2)}, u32[]{:S(2)}) %all-to-all-start.21) | async-done | bytes 2097184 | tf_op jit(solution)/shard_map/all_to_all | solution.py:398
  95.1 81.7 %conditional.2 = (bf16[16,16,16,256]{3,2,1,0:T(8,128)(2,1)S(1)}) conditional(s32[]{:T(128)} %clamp.7, (bf16[16,256,256]{2,1,0:T(8,128)(2,1)S(1)}, s32[1]{0:T(128)}, s32[16,1,256]{2,1,0:T(1,128)S(1)}) %tuple.80, (bf16[16,256,256]{2,1,0:T(8,128)(2,1)S(1)}, s32[1]{0:T(128)}, s32[16,1,256]{2,1,0:T(1,128)S(1)}) %tuple.80, ...), branch_computations={%region_10.11_spmd, %region_11.12_spmd, %region_12.13_spmd, %regio... | conditional | bytes 4194312 | solution.py:424
  95.1 1.7 branch_5_fun.4
  96.8 76.4 %all_to_all.100.rows = bf16[16,184,256]{2,1,0:T(8,128)(2,1)S(1)} all-to-all(bf16[16,184,256]{2,1,0:T(8,128)(2,1)S(1)} %branch_5_fun.4), channel_id=1, replica_groups={{0,2,4,6,8,10,12,14,16,18,20,22,24,26,28,30},{1,3,5,7,9,11,13,15,17,19,..., dimensions={0} | all-to-all | bytes 3014656 | tf_op jit(solution)/shard_map/cond/branch_5_fun/all_to_all | solution.py:313
  173.3 3.5 %branch_5_fun.5 = bf16[16,16,16,256]{3,2,1,0:T(8,128)(2,1)S(1)} custom-call(bf16[16,184,256]{2,1,0:T(8,128)(2,1)S(1)} %all_to_all.100.rows, s32[16,1,256]{2,1,0:T(1,128)S(1)} %get-tuple-element.185.place), custom_call_target="tpu_custom_call" | custom-call | tf_op jit(solution)/shard_map/cond/branch_5_fun/pallas_call | solution.py:246
  176.8 80.2 %conditional.3 = (bf16[16,16,16,256]{3,2,1,0:T(8,128)(2,1)S(1)}) conditional(s32[]{:T(128)} %clamp.6, (s32[256]{0:T(256)S(1)}, bf16[16,16,16,256]{3,2,1,0:T(8,128)(2,1)S(1)}, s32[16,1,256]{2,1,0:T(1,128)S(1)}, s32[1]{0:T(128)}) %tuple.81, (s32[256]{0:T(256)S(1)}, bf16[16,16,16,256]{3,2,1,0:T(8,128)(2,1)S(1)}, ...), branch_computations={%region_20.21_spmd, %region_21.22_spmd, %region_22.23_spmd, %regio... | conditional | bytes 4194312 | solution.py:424
  176.9 3.7 %branch_4_fun.6 = bf16[16,176,256]{2,1,0:T(8,128)(2,1)S(1)} custom-call(s32[256]{0:T(256)S(1)} %get-tuple-element.215.source, bf16[16,16,16,256]{3,2,1,0:T(8,128)(2,1)S(1)} %get-tuple-element.216.rows, s32[16,1,256]{2,1,0:T(1,128)S(1)} %get-tuple-element.217.place), custom_call_target="tpu_custom_call" | custom-call | tf_op jit(solution)/shard_map/cond/branch_4_fun/pallas_call | solution.py:246
  180.6 74.2 %all_to_all.109.rows = bf16[16,176,256]{2,1,0:T(8,128)(2,1)S(1)} all-to-all(bf16[16,176,256]{2,1,0:T(8,128)(2,1)S(1)} %branch_4_fun.6), channel_id=1, replica_groups={{0,2,4,6,8,10,12,14,16,18,20,22,24,26,28,30},{1,3,5,7,9,11,13,15,17,19,..., dimensions={0} | all-to-all | bytes 2883584 | tf_op jit(solution)/shard_map/cond/branch_4_fun/all_to_all | solution.py:313
  254.8 2.0 branch_4_fun.7
  257.0 1.3 copy-done.1
  258.3 5.3 %all-to-all-start.22 = ((bf16[16,256,256]{2,1,0:T(8,128)(2,1)}), bf16[16,256,256]{2,1,0:T(8,128)(2,1)S(1)}, u32[]{:S(2)}, u32[]{:S(2)}) async-start(bf16[16,256,256]{2,1,0:T(8,128)(2,1)} %bitcast.41), calls=%async_computation.22 | async-start | bytes 4194304 | tf_op jit(solution)/shard_map/all_to_all | solution.py:428
  264.2 0.6 dynamic_slice.18
  265.3 0.1 pad_add_fusion.sc
  265.4 20.9 %all-to-all-done.22.rows = bf16[16,256,256]{2,1,0:T(8,128)(2,1)S(1)} async-done(((bf16[16,256,256]{2,1,0:T(8,128)(2,1)}), bf16[16,256,256]{2,1,0:T(8,128)(2,1)S(1)}, u32[]{:S(2)}, u32[]{:S(2)}) %all-to-all-start.22) | async-done | bytes 2097184 | tf_op jit(solution)/shard_map/all_to_all | solution.py:428
  286.3 2.6 shard_map.156
  288.9 11.0 %collective-permute-start.4 = (bf16[128,4096]{1,0:T(8,128)(2,1)S(1)}, bf16[128,4096]{1,0:T(8,128)(2,1)S(1)}, u32[]{:S(2)}, u32[]{:S(2)}) collective-permute-start(bf16[128,4096]{1,0:T(8,128)(2,1)S(1)} %get-tuple-element.257), channel_id=1, source_target_pairs={{0,1},{1,0},{2,3},{3,2},{4,5},{5,4},{6,7},{7,6},{8,9},{9,8},{10,11... | collective-permute-start | bytes 3145736 | tf_op jit(solution)/shard_map/ppermute | solution.py:437
  300.0 2.3 collective-permute-done.4.oth
  302.2 3.1 %norm.1 = bf16[128,8192]{1,0:T(8,128)(2,1)} custom-call(s32[3]{0:T(128)S(1)} %pad_add_fusion.sc, bf16[128,4096]{1,0:T(8,128)(2,1)S(1)} %get-tuple-element.256.own, bf16[128,4096]{1,0:T(8,128)(2,1)S(1)} %collective-permute-done.4.oth, f32[1,8192]{1,0:T(1,128)S(1)} %bitcast.30), custom_call_target="tpu_custom_call" | custom-call | tf_op jit(solution)/shard_map/norm/pallas_call | solution.py:439
  (40 shorter events, 0.4 us)
Async XLA Ops:
  0.0 12.8 %copy-start.4 = (bf16[128,128]{1,0:T(8,128)(2,1)S(1)}, bf16[128,128]{1,0:T(8,128)(2,1)}, u32[]{:S(2)}) copy-start(bf16[128,128]{1,0:T(8,128)(2,1)} %param.38) | copy-start | bytes 98308
  0.0 14.9 %copy-start.5 = (bf16[128,256]{1,0:T(8,128)(2,1)S(1)}, bf16[128,256]{1,0:T(8,128)(2,1)}, u32[]{:S(2)}) copy-start(bf16[128,256]{1,0:T(8,128)(2,1)} %bc_own.1) | copy-start | bytes 196612
  0.0 17.3 %copy-start.8 = (s32[256]{0:T(256)S(1)}, s32[256]{0:T(256)}, u32[]{:S(2)}) copy-start(s32[256]{0:T(256)} %param.47) | copy-start | bytes 3076
  0.0 18.5 %copy-start.10 = (f32[256]{0:T(256)S(1)}, f32[256]{0:T(256)}, u32[]{:S(2)}) copy-start(f32[256]{0:T(256)} %param.45) | copy-start | bytes 3076
  0.0 18.5 %copy-start.7 = (f32[4,256]{1,0:T(4,128)S(1)}, f32[4,256]{1,0:T(4,128)}, u32[]{:S(2)}) copy-start(f32[4,256]{1,0:T(4,128)} %param.44) | copy-start | bytes 12292
  0.0 20.4 %copy-start.13 = (f32[128]{0:T(128)S(1)}, f32[128]{0:T(128)}, u32[]{:S(2)}) copy-start(f32[128]{0:T(128)} %param.39) | copy-start | bytes 1540
  1.5 19.0 %collective-permute-start.1 = (f32[8,256]{1,0:T(8,128)}, f32[8,256]{1,0:T(8,128)S(1)}, u32[]{:S(2)}, u32[]{:S(2)}) collective-permute-start(f32[8,256]{1,0:T(8,128)} %shard_map.154), channel_id=1, source_target_pairs={{0,0},{1,2},{2,4},{3,6},{4,8},{5,10},{6,12},{7,14},{8,16},{9,18},{... | collective-permute-start | bytes 24584 | tf_op jit(solution)/shard_map/ppermute | solution.py:310
  7.7 39.0 %collective-permute-start = (bf16[128,4096]{1,0:T(8,128)(2,1)S(1)}, bf16[128,4096]{1,0:T(8,128)(2,1)S(1)}, u32[]{:S(2)}, u32[]{:S(2)}) collective-permute-start(bf16[128,4096]{1,0:T(8,128)(2,1)S(1)} %constant_dynamic-slice_fusion.1), channel_id=1, source_target_pairs={{0,1},{1,0},{2,3},{3,2},{4,5},{5,4},{6,7},{7,6},{8,9},{9,8},{10,11... | collective-permute-start | bytes 3145736 | tf_op jit(solution)/shard_map/ppermute | solution.py:292
  12.9 21.8 %collective-permute-start.3 = (bf16[128,64]{1,0:T(8,128)(2,1)S(1)}, bf16[128,64]{1,0:T(8,128)(2,1)S(1)}, u32[]{:S(2)}, u32[]{:S(2)}) collective-permute-start(bf16[128,64]{1,0:T(8,128)(2,1)S(1)} %constant_dynamic-slice_fusion), channel_id=1, source_target_pairs={{0,1},{1,0},{2,3},{3,2},{4,5},{5,4},{6,7},{7,6},{8,9},{9,8},{10,11... | collective-permute-start | bytes 49160 | tf_op jit(solution)/shard_map/ppermute | solution.py:296
  14.9 20.8 %collective-permute-start.2 = (bf16[128,256]{1,0:T(8,128)(2,1)S(1)}, bf16[128,256]{1,0:T(8,128)(2,1)S(1)}, u32[]{:S(2)}, u32[]{:S(2)}) collective-permute-start(bf16[128,256]{1,0:T(8,128)(2,1)S(1)} %copy-done.5), channel_id=1, source_target_pairs={{0,1},{1,0},{2,3},{3,2},{4,5},{5,4},{6,7},{7,6},{8,9},{9,8},{10,11... | collective-permute-start | bytes 196616 | tf_op jit(solution)/shard_map/ppermute | solution.py:295
  21.1 25.5 %all-to-all-start.20 = ((f32[16,8,256]{2,1,0:T(8,128)}), f32[16,8,256]{2,1,0:T(8,128)S(1)}, u32[]{:S(2)}, u32[]{:S(2)}) async-start(f32[16,8,256]{2,1,0:T(8,128)} %broadcast_in_dim.77), calls=%async_computation.20 | async-start | bytes 262144 | tf_op jit(solution)/shard_map/all_to_all | solution.py:313
  35.7 0.6 copy-start.6
  46.7 0.6 copy-start.3
  46.7 1.0 copy-start.2
  63.4 6.9 %copy-start.9 = (s32[256]{0:T(256)S(1)}, s32[256]{0:T(256)}, u32[]{:S(2)}) copy-start(s32[256]{0:T(256)} %param.48) | copy-start | bytes 3076
  63.4 7.0 %copy-start.11 = (s32[256]{0:T(256)S(1)}, s32[256]{0:T(256)}, u32[]{:S(2)}) copy-start(s32[256]{0:T(256)} %param.49) | copy-start | bytes 3076
  63.4 9.1 %copy-start.12 = (s32[9]{0:T(128)S(1)}, s32[9]{0:T(128)}, u32[]{:S(2)}) copy-start(s32[9]{0:T(128)} %constant.113.clone) | copy-start | bytes 112
  63.4 31.7 %all-to-all-start.21 = ((bf16[16,256,256]{2,1,0:T(8,128)(2,1)}), bf16[16,256,256]{2,1,0:T(8,128)(2,1)S(1)}, u32[]{:S(2)}, u32[]{:S(2)}) async-start(bf16[16,256,256]{2,1,0:T(8,128)(2,1)} %mix.1), calls=%async_computation.21 | async-start | bytes 4194304 | tf_op jit(solution)/shard_map/all_to_all | solution.py:398
  257.0 1.3 copy-start.1
  258.3 28.0 %all-to-all-start.22 = ((bf16[16,256,256]{2,1,0:T(8,128)(2,1)}), bf16[16,256,256]{2,1,0:T(8,128)(2,1)S(1)}, u32[]{:S(2)}, u32[]{:S(2)}) async-start(bf16[16,256,256]{2,1,0:T(8,128)(2,1)} %bitcast.41), calls=%async_computation.22 | async-start | bytes 4194304 | tf_op jit(solution)/shard_map/all_to_all | solution.py:428
  263.6 38.6 %copy-start = (f32[8192]{0:T(1024)S(1)}, f32[8192]{0:T(1024)}, u32[]{:S(2)}) copy-start(f32[8192]{0:T(1024)} %param.46) | copy-start | bytes 98308
  288.9 13.3 %collective-permute-start.4 = (bf16[128,4096]{1,0:T(8,128)(2,1)S(1)}, bf16[128,4096]{1,0:T(8,128)(2,1)S(1)}, u32[]{:S(2)}, u32[]{:S(2)}) collective-permute-start(bf16[128,4096]{1,0:T(8,128)(2,1)S(1)} %get-tuple-element.257), channel_id=1, source_target_pairs={{0,1},{1,0},{2,3},{3,2},{4,5},{5,4},{6,7},{7,6},{8,9},{9,8},{10,11... | collective-permute-start | bytes 3145736 | tf_op jit(solution)/shard_map/ppermute | solution.py:437
